TPU v7x, 128 devices: a whole 4x4x4 slice. The times are simulated.
128 devices in a mesh: row: 8 (over z, core), col: 16 (over y, x).
Axes of the slice: x: 4, y: 4, z: 4, core: 2. Of those that a mesh axis runs over, the one named last changes fastest.
Arguments:
- front_diag: float32 [1024, 1024], replicated, may hold values from -4 to 16, as said below
- panel_rows: float32 [16384, 1024], P(('row', 'col')), may hold values from -1.2 to 1.2
- trailing: float32 [16384, 16384], P('row', 'col'), may hold values from -6 to 6
- pattern: int32 [64, 64], P('row', 'col'), may hold values 0 or 1
Outputs:
- diag_factor: float32 [1024, 1024], replicated
- panel_factor: float32 [16384, 1024], P(('row', 'col'))
- schur: float32 [16384, 16384], P('row', 'col')
Inputs may be any that keep to these rules, and one draw needn't show every extreme that they name: front_diag is symmetric and positive definite, with smallest eigenvalue at least 0.5.
All inputs are finite; a program needn't handle non-finite values. No bound on the sum of `pattern` on one device may be relied on, other than what follows from the above.
Results may differ from a plain program's by a relative error of at most 0.0003.
Values sent between devices are 32-bit elements; how exact they have to be, the bound alone decides.
A program may use at most 128 MiB of HBM per device.

v0:
```python
import jax
import jax.numpy as jnp
from jax import lax
from jax.sharding import PartitionSpec as P

BLOCK = 256


def spread(block, axis, holder):
    block = jnp.where(lax.axis_index(axis) == holder, block, jnp.zeros_like(block))
    return lax.psum(block, axis)


def column_rows(row_part, col_rows):
    ratio = lax.axis_size("col") // lax.axis_size("row")
    offset = lax.axis_index("col") % ratio * col_rows
    return lax.dynamic_slice_in_dim(row_part, offset, col_rows, 0)


def local(front_diag, panel_rows, trailing, pattern):
    diag_factor = jnp.linalg.cholesky(front_diag)
    panel_factor = jax.scipy.linalg.solve_triangular(diag_factor, panel_rows.T, lower=True).T
    local_rows = trailing.shape[0]
    col_rows = trailing.shape[1]
    ratio = lax.axis_size("col") // lax.axis_size("row")
    root_row = lax.axis_index("col") // ratio
    row_part = lax.all_gather(panel_factor, "col", axis=0, tiled=True)
    piece = column_rows(row_part, col_rows)
    col_part = spread(piece, "row", root_row)
    update = jnp.dot(row_part, col_part.T, precision=lax.Precision.HIGHEST)
    row_blocks = local_rows // BLOCK
    col_blocks = col_rows // BLOCK
    row_index = lax.axis_index("row") * row_blocks + jnp.arange(row_blocks)
    col_index = lax.axis_index("col") * col_blocks + jnp.arange(col_blocks)
    lower = (row_index[:, None] >= col_index[None, :]).astype(jnp.float32)
    keep = pattern.astype(jnp.float32) * lower
    masked = update.reshape(row_blocks, BLOCK, col_blocks, BLOCK) * keep[:, None, :, None]
    schur = trailing - masked.reshape(local_rows, col_rows)
    return (diag_factor, panel_factor, schur)


def solution(mesh):
    return jax.shard_map(
        local,
        mesh=mesh,
        in_specs=(P(), P(("row", "col"), None), P("row", "col"), P("row", "col")),
        out_specs=(P(), P(("row", "col"), None), P("row", "col")),
        check_vma=False,
    )
```

profile of v0, /device:TPU:0, one launch (start us, length us, event | category | flops | bytes accessed | tf_op | source)
XLA Modules:
  0.0 537.7 jit_solution(12177218288238149050)
XLA Ops:
  7.2 5.3 copy.7
  12.6 4.4 fusion
  19.0 11.7 %cholesky.223 = f32[128,128]{1,0:T(8,128)S(1)} custom-call(f32[128,128]{1,0:T(8,128)S(1)} %cholesky.580), custom_call_target="Cholesky" | custom-call | tf_op jit(solution)/shard_map/jit(cholesky)/cholesky | solution.py:21
  30.8 9.8 %custom-call.63 = f32[1,128,128]{1,2,0:T(8,128)S(1)} custom-call(f32[1,128,128]{2,1,0:T(8,128)S(1)} %get-tuple-element.61), custom_call_target="InvertDiagBlocksLowerTriangular" | custom-call | tf_op jit(solution)/shard_map/jit(cholesky)/cholesky | solution.py:21
  40.6 2.5 cholesky.255
  43.1 2.3 constant_dynamic-update-slice_fusion.32
  47.0 11.9 %cholesky.244 = f32[128,128]{1,0:T(8,128)S(1)} custom-call(f32[128,128]{1,0:T(8,128)S(1)} %cholesky.584), custom_call_target="Cholesky" | custom-call | tf_op jit(solution)/shard_map/jit(cholesky)/cholesky | solution.py:21
  59.5 9.8 %custom-call.64 = f32[1,128,128]{1,2,0:T(8,128)S(1)} custom-call(f32[1,128,128]{2,1,0:T(8,128)S(1)} %get-tuple-element.58), custom_call_target="InvertDiagBlocksLowerTriangular" | custom-call | tf_op jit(solution)/shard_map/jit(cholesky)/cholesky | solution.py:21
  72.7 11.7 %cholesky.468 = f32[128,128]{1,0:T(8,128)S(1)} custom-call(f32[128,128]{1,0:T(8,128)S(1)} %cholesky.589), custom_call_target="Cholesky" | custom-call | tf_op jit(solution)/shard_map/jit(cholesky)/cholesky | solution.py:21
  85.7 9.8 %custom-call.65 = f32[1,128,128]{1,2,0:T(8,128)S(1)} custom-call(f32[1,128,128]{2,1,0:T(8,128)S(1)} %get-tuple-element.55), custom_call_target="InvertDiagBlocksLowerTriangular" | custom-call | tf_op jit(solution)/shard_map/jit(cholesky)/cholesky | solution.py:21
  96.6 2.3 convolution_subtract_fusion.2
  99.0 11.9 %cholesky.487 = f32[128,128]{1,0:T(8,128)S(1)} custom-call(f32[128,128]{1,0:T(8,128)S(1)} %cholesky.594), custom_call_target="Cholesky" | custom-call | tf_op jit(solution)/shard_map/jit(cholesky)/cholesky | solution.py:21
  112.2 9.8 %custom-call.66 = f32[1,128,128]{1,2,0:T(8,128)S(1)} custom-call(f32[1,128,128]{2,1,0:T(8,128)S(1)} %get-tuple-element.52), custom_call_target="InvertDiagBlocksLowerTriangular" | custom-call | tf_op jit(solution)/shard_map/jit(cholesky)/cholesky | solution.py:21
  123.1 2.4 convolution_subtract_fusion.3
  125.4 11.7 %cholesky.506 = f32[128,128]{1,0:T(8,128)S(1)} custom-call(f32[128,128]{1,0:T(8,128)S(1)} %cholesky.599), custom_call_target="Cholesky" | custom-call | tf_op jit(solution)/shard_map/jit(cholesky)/cholesky | solution.py:21
  138.5 10.2 %custom-call.67 = f32[1,128,128]{1,2,0:T(8,128)S(1)} custom-call(f32[1,128,128]{2,1,0:T(8,128)S(1)} %get-tuple-element.49), custom_call_target="InvertDiagBlocksLowerTriangular" | custom-call | tf_op jit(solution)/shard_map/jit(cholesky)/cholesky | solution.py:21
  149.7 2.3 convolution_subtract_fusion.4
  152.0 11.7 %cholesky.526 = f32[128,128]{1,0:T(8,128)S(1)} custom-call(f32[128,128]{1,0:T(8,128)S(1)} %cholesky.604), custom_call_target="Cholesky" | custom-call | tf_op jit(solution)/shard_map/jit(cholesky)/cholesky | solution.py:21
  165.0 9.8 %custom-call.68 = f32[1,128,128]{1,2,0:T(8,128)S(1)} custom-call(f32[1,128,128]{2,1,0:T(8,128)S(1)} %get-tuple-element.46), custom_call_target="InvertDiagBlocksLowerTriangular" | custom-call | tf_op jit(solution)/shard_map/jit(cholesky)/cholesky | solution.py:21
  177.9 11.9 %cholesky.546 = f32[128,128]{1,0:T(8,128)S(1)} custom-call(f32[128,128]{1,0:T(8,128)S(1)} %cholesky.609), custom_call_target="Cholesky" | custom-call | tf_op jit(solution)/shard_map/jit(cholesky)/cholesky | solution.py:21
  191.0 9.8 %custom-call.69 = f32[1,128,128]{1,2,0:T(8,128)S(1)} custom-call(f32[1,128,128]{2,1,0:T(8,128)S(1)} %get-tuple-element.43), custom_call_target="InvertDiagBlocksLowerTriangular" | custom-call | tf_op jit(solution)/shard_map/jit(cholesky)/cholesky | solution.py:21
  203.4 11.7 %cholesky.564 = f32[128,128]{1,0:T(8,128)S(1)} custom-call(f32[128,128]{1,0:T(8,128)S(1)} %convolution_subtract_fusion.11), custom_call_target="Cholesky" | custom-call | tf_op jit(solution)/shard_map/jit(cholesky)/cholesky | solution.py:21
  222.0 6.8 %fusion.1 = (f32[1024,1024]{1,0:T(8,128)}, f32[1024,1024]{1,0:T(8,128)}) fusion(f32[1024,1024]{1,0:T(8,128)} %get-tuple-element.41, pred[]{:T(512)S(6)} %cholesky.579), kind=kLoop, calls=%fused_computation.8 | loop fusion | flops 4194304 | bytes 12582913 | tf_op jit(solution)/shard_map/jit(_solve_triangular)/triangular_solve | solution.py:22
  228.8 22.5 %while.1 = (s32[]{:T(128)}, f32[1024,1024]{1,0:T(8,128)}, s32[8,2]{0,1:T(2,128)S(1)}, f32[8,128,128]{2,1,0:T(8,128)S(1)}, s32[]{:T(128)}) while((s32[]{:T(128)}, f32[1024,1024]{1,0:T(8,128)}, s32[8,2]{0,1:T(2,128)S(1)}, f32[8,128,128]{2,1,0:T(8,128)S(1)}, s32[]{:T(128)}) %tuple.58), condition=%wide.while_cond, body=%wide.while_body.sunk | while | flops 2 | bytes 131189 | solution.py:22
  229.4 2.2 bitcast_dynamic-update-slice_fusion.2
  232.3 2.2 bitcast_dynamic-update-slice_fusion.2
  251.3 78.8 %custom-call.70 = f32[8,128,128]{1,2,0:T(8,128)S(1)} custom-call(f32[8,128,128]{2,1,0:T(8,128)S(1)} %get-tuple-element.10), custom_call_target="InvertDiagBlocksLowerTriangular" | custom-call | tf_op jit(solution)/shard_map/jit(_solve_triangular)/triangular_solve | solution.py:22
  344.9 73.2 %all-gather.2.cloned.1.call-done = f32[2048,1024]{1,0:T(8,128)} async-done(((f32[128,1024]{1,0:T(8,128)}), f32[2048,1024]{1,0:T(8,128)}) %all-gather.2.cloned.1.call-update) | async-done | bytes 8388624 | tf_op jit(solution)/shard_map/all_gather | solution.py:27
  418.1 5.0 dynamic-slice_select_fusion
  425.0 5.5 %copy.18 = f32[256,8,4,256]{3,1,2,0:T(8,128)} copy(f32[256,8,4,256]{3,2,1,0:T(4,128)S(1)} %bitcast.109) | data formatting | bytes 16777216
  430.5 65.2 %all-reduce.3.cloned.1.call-done = f32[1024,1024]{1,0:T(8,128)} async-done(((f32[1024,1024]{1,0:T(8,128)}), f32[1024,1024]{1,0:T(8,128)}) %all-reduce.3.cloned.1.call-update) | async-done | bytes 4194320 | tf_op jit(solution)/shard_map/psum | solution.py:11
  495.8 34.7 %multiply_subtract_fusion = f32[2048,1024]{1,0:T(8,128)} fusion(f32[2048,1024]{1,0:T(8,128)} %param.6, f32[2048,1024]{1,0:T(8,128)} %bitcast.108, f32[2048,1024]{1,0:T(8,128)} %all-gather.2.cloned.1.call-done, f32[1024,1024]{1,0:T(8,128)} %all-reduce.3.cloned.1.call-done), kind=kOutput, calls=%fused_computation.2 | convolution fusion | flops 25773998080 | bytes 37748736 | tf_op jit(solution)/shard_map/dot_general | solution.py:30
  (103 shorter events, 59.3 us)
Async XLA Ops:
  7.2 410.9 %all-gather.2.cloned.1.call-start = ((), (), s32[]{:S(2)}) async-start(), calls=%async_computation | async-start | bytes 8912896 | tf_op jit(solution)/shard_map/all_gather | solution.py:27
  17.0 2.0 copy-start
  222.0 108.2 %copy-start.2 = (f32[128,1024]{1,0:T(8,128)S(1)}, f32[128,1024]{1,0:T(8,128)}, u32[]{:S(2)}) copy-start(f32[128,1024]{1,0:T(8,128)} %param.5) | copy-start | bytes 1572868
  344.0 0.8 copy-start.1
  344.8 150.9 %all-reduce.3.cloned.1.call-start = ((), (), s32[]{:S(2)}) async-start(), calls=%async_computation.1 | async-start | bytes 8388608 | tf_op jit(solution)/shard_map/psum | solution.py:11
  423.1 0.7 copy-start.3
Sparse Core Ops, SparseCore 0:
  345.0 73.0 all-gather.1
  423.2 72.5 all-reduce.2
where the time goes:
time: 548 us; the launch traced here: 538 us
  other arithmetic  267 us (49%)
  waiting for transfers between devices  138 us (25%)
  matrix products  70.7 us (13%)
  local copies, waits for them, and re-layouts  41.1 us (8%)
  between operations  19.9 us (4%)
    another operation x30, other arithmetic, local(): diag_factor = jnp.linalg.cholesky(front_diag)  172 us
    another operation x3, other arithmetic, local(): jax.scipy.linalg.solve_triangular(diag_factor, panel_rows.T, lower=True)  85.7 us
    all_gather x1, waiting for transfers between devices, local(): row_part = lax.all_gather(panel_factor, 'col', axis=0, tiled=True)  73.2 us
    psum x1, waiting for transfers between devices, spread(): return lax.psum(block, axis)  65.2 us
    dot_general x1, matrix products, local(): update = jnp.dot(row_part, col_part.T, precision=lax.Precision.HIGHEST)  34.7 us
    another operation x14, matrix products, local(): diag_factor = jnp.linalg.cholesky(front_diag)  23 us
    another operation x24, local copies, waits for them, and re-layouts  22.4 us
    unnamed x17, local copies, waits for them, and re-layouts  14.3 us
  transfers between devices with their start and end apart: 2, of which 2 were waited for; matrix products, arithmetic and copies ran while one was open for 1% of the time, Pallas kernels for 0%

commit v1 on v0

v1 whole, which is shorter than its diff:
```python
import jax
import jax.numpy as jnp
from jax import lax
from jax.experimental import pallas as pl
from jax.experimental.pallas import tpu as pltpu
from jax.sharding import PartitionSpec as P

BLOCK = 256
HI = lax.Precision.HIGHEST


def factor_tile(s, t):
    sub = lax.broadcasted_iota(jnp.int32, (8, 128), 0)
    def wide(x, c):
        return jnp.broadcast_to(x[:, c:c + 1], (8, 128))
    def tall(x, k):
        return jnp.broadcast_to(x[k:k + 1, :], (8, 128))
    n = len(s)
    for g in range(n):
        r, q = s[g], t[g]
        c = [wide(r, 8 * g + m) for m in range(8)]
        u = jnp.zeros((8, 128), jnp.float32)
        w = u
        for k in range(8):
            here = sub == k
            f = c[k]
            p = tall(f, k)
            inv = 1.0 / p
            root = lax.rsqrt(p)
            rk, qk = tall(r, k), tall(q, k)
            u = jnp.where(here, rk * root, u)
            w = jnp.where(here, qk * root, w)
            r = jnp.where(here, rk * inv, r - (f * rk) * inv)
            q = jnp.where(here, qk * inv, q - (f * qk) * inv)
            for m in range(k + 1, 8):
                cm = tall(c[m], k)
                c[m] = jnp.where(here, cm * inv, c[m] - (f * cm) * inv)
        for h in range(g + 1, n):
            sh, th = s[h], t[h]
            ds, dt = None, None
            for m in range(8):
                b = wide(s[h], 8 * g + m)
                a1, a2 = b * tall(r, m), b * tall(q, m)
                ds = a1 if ds is None else ds + a1
                dt = a2 if dt is None else dt + a2
            s[h], t[h] = sh - ds, th - dt
        s[g], t[g] = u, w
    return s, t

def chol_kernel(a_ref, l_ref, w_ref, g_ref, u_ref, wd_ref):
    n = a_ref.shape[0]
    nb = n // 128
    w_ref[...] = a_ref[...]
    l_ref[...] = jnp.zeros_like(l_ref)
    sub = lax.broadcasted_iota(jnp.int32, (8, 128), 0)
    lane = lax.broadcasted_iota(jnp.int32, (8, 128), 1)
    lane_all = lax.broadcasted_iota(jnp.int32, (128, n), 1)

    def panel(p, carry):
        o = pl.multiple_of(p * 128, 128)
        s = [w_ref[pl.ds(o + 8 * g, 8), pl.ds(o, 128)] for g in range(16)]
        t = [(lane == sub + 8 * g).astype(jnp.float32) for g in range(16)]
        s, t = factor_tile(s, t)
        for g in range(16):
            u_ref[8 * g:8 * g + 8, :] = jnp.where(lane >= sub + 8 * g, s[g], 0.0)
            wd_ref[8 * g:8 * g + 8, :] = t[g]
        wd = wd_ref[...]
        rows = w_ref[pl.ds(o, 128), :]
        g_ref[...] = jnp.dot(wd, rows, precision=HI, preferred_element_type=jnp.float32)
        g_ref[:, pl.ds(o, 128)] = wd
        w_ref[pl.ds(o, 128), :] = jnp.where(lane_all < o + 128, g_ref[...], 0.0)
        l_ref[pl.ds(o, 128), pl.ds(o, 128)] = u_ref[...].T

        def below(i, c):
            oi = pl.multiple_of(i * 128, 128)
            li = g_ref[:, pl.ds(oi, 128)].T
            l_ref[pl.ds(oi, 128), pl.ds(o, 128)] = li
            w_ref[pl.ds(oi, 128), pl.ds(o, 128)] = jnp.zeros((128, 128), jnp.float32)
            w_ref[pl.ds(oi, 128), :] -= jnp.dot(li, g_ref[...], precision=HI, preferred_element_type=jnp.float32)
            return c
        lax.fori_loop(p + 1, nb, below, 0)
        return carry
    lax.fori_loop(0, nb, panel, 0)

def chol(a):
    n = a.shape[0]
    f32 = jnp.float32
    return pl.pallas_call(
        chol_kernel,
        out_shape=(jax.ShapeDtypeStruct((n, n), f32),) * 2,
        in_specs=[pl.BlockSpec(memory_space=pltpu.VMEM)],
        out_specs=(pl.BlockSpec(memory_space=pltpu.VMEM),) * 2,
        scratch_shapes=[pltpu.VMEM((128, n), f32), pltpu.VMEM((128, 128), f32), pltpu.VMEM((128, 128), f32)],
        compiler_params=pltpu.CompilerParams(vmem_limit_bytes=60 << 20),
        name="factor",
    )(a)

NT = (((1,), (1,)), ((), ()))
NN = (((1,), (0,)), ((), ()))


def halves(x):
    high = x.astype(jnp.bfloat16)
    return high, (x - high.astype(jnp.float32)).astype(jnp.bfloat16)


def dot3(a, b, dims):
    def one(x, y):
        return lax.dot_general(x, y, dims, preferred_element_type=jnp.float32)
    return one(a[0], b[0]) + (one(a[0], b[1]) + one(a[1], b[0]))


def apply_kernel(w_ref, own_ref, c_ref, x_ref, yh_ref, yl_ref, wh, wl, ch, cl, zh, zl):
    n = w_ref.shape[0]
    wh[...], wl[...] = halves(w_ref[...])
    ch[...], cl[...] = halves(c_ref[...])
    x_ref[...] = lax.dot_general(own_ref[...], w_ref[...], NT, precision=HI, preferred_element_type=jnp.float32)
    for p in range(0, n, BLOCK):
        e = p + BLOCK
        z = dot3((ch[:, :e], cl[:, :e]), (wh[p:e, :e], wl[p:e, :e]), NT)
        zh[:, p:e], zl[:, p:e] = halves(z)
    for p in range(0, n, BLOCK):
        e = p + BLOCK
        y = dot3((zh[:, p:], zl[:, p:]), (wh[p:, p:e], wl[p:, p:e]), NN)
        yh_ref[:, p:e], yl_ref[:, p:e] = halves(y)


def apply_inverse(w, own, c):
    f32, bf = jnp.float32, jnp.bfloat16
    n, m = w.shape[0], c.shape[0]
    vm = pl.BlockSpec(memory_space=pltpu.VMEM)
    return pl.pallas_call(
        apply_kernel,
        out_shape=(jax.ShapeDtypeStruct(own.shape, f32), jax.ShapeDtypeStruct((m, n), bf), jax.ShapeDtypeStruct((m, n), bf)),
        in_specs=[vm] * 3,
        out_specs=(vm,) * 3,
        scratch_shapes=[pltpu.VMEM((n, n), bf)] * 2 + [pltpu.VMEM((m, n), bf)] * 4,
        compiler_params=pltpu.CompilerParams(vmem_limit_bytes=60 << 20),
        name="apply",
    )(w, own, c)


def update_kernel(keep_ref, r_ref, yh_ref, yl_ref, t_ref, o_ref, rh, rl):
    i = pl.program_id(0)
    cols = o_ref.shape[1] // BLOCK
    rh[...], rl[...] = halves(r_ref[...])
    for j in range(cols):
        part = slice(j * BLOCK, (j + 1) * BLOCK)
        kept = keep_ref[i * cols + j] != 0

        @pl.when(kept)
        def _():
            d = dot3((rh[...], rl[...]), (yh_ref[part, :], yl_ref[part, :]), NT)
            o_ref[:, part] = t_ref[:, part] - d

        @pl.when(jnp.logical_not(kept))
        def _():
            o_ref[:, part] = t_ref[:, part]


def update(keep, rows, yh, yl, trailing):
    m, n = trailing.shape
    k = rows.shape[1]
    return pl.pallas_call(
        update_kernel,
        out_shape=jax.ShapeDtypeStruct((m, n), jnp.float32),
        grid_spec=pltpu.PrefetchScalarGridSpec(
            num_scalar_prefetch=1,
            grid=(m // BLOCK,),
            in_specs=[
                pl.BlockSpec((BLOCK, k), lambda i, s: (i, 0)),
                pl.BlockSpec((n, k), lambda i, s: (0, 0)),
                pl.BlockSpec((n, k), lambda i, s: (0, 0)),
                pl.BlockSpec((BLOCK, n), lambda i, s: (i, 0)),
            ],
            out_specs=pl.BlockSpec((BLOCK, n), lambda i, s: (i, 0)),
            scratch_shapes=[pltpu.VMEM((BLOCK, k), jnp.bfloat16)] * 2,
        ),
        compiler_params=pltpu.CompilerParams(vmem_limit_bytes=60 << 20),
        name="update",
    )(keep, rows, yh, yl, trailing)


def local(front_diag, panel_rows, trailing, pattern):
    nrow, ncol = lax.axis_size("row"), lax.axis_size("col")
    ratio = ncol // nrow
    pairs = []
    for c in range(ncol):
        for r in range(nrow):
            pairs.append(((c // ratio) * ncol + (c % ratio) * nrow + r, r * ncol + c))
    rows = lax.all_gather(panel_rows, "col", axis=0, tiled=True)
    piece = lax.ppermute(panel_rows, ("row", "col"), pairs)
    col_rows = lax.all_gather(piece, "row", axis=0, tiled=True)
    diag_factor, inverse = chol(front_diag)
    panel_factor, yh, yl = apply_inverse(inverse, panel_rows, col_rows)
    row_blocks, col_blocks = pattern.shape
    row_index = lax.axis_index("row") * row_blocks + jnp.arange(row_blocks)
    col_index = lax.axis_index("col") * col_blocks + jnp.arange(col_blocks)
    keep = pattern * (row_index[:, None] >= col_index[None, :]).astype(jnp.int32)
    schur = update(keep.reshape(-1), rows, yh, yl, trailing)
    return (diag_factor, panel_factor, schur)


def solution(mesh):
    return jax.shard_map(
        local,
        mesh=mesh,
        in_specs=(P(), P(("row", "col"), None), P("row", "col"), P("row", "col")),
        out_specs=(P(), P(("row", "col"), None), P("row", "col")),
        check_vma=False,
    )
```

time: 548 us -> 195 us (0.36)
  the two profiles are of different devices: /device:TPU:0 before, /device:TPU:37 now
where the time goes in v1:
time: 195 us; the launch traced here: 194 us
  Pallas kernels  106 us (54%)
  waiting for transfers between devices  69 us (35%)
  between operations  14.1 us (7%)
  starting transfers between devices  3.85 us (2%)
    pallas_call x1, Pallas kernels, chol(): pl.pallas_call(chol_kernel, out_shape=(jax.ShapeDtypeStruct((n, n), f32),...  64.9 us
    all_gather x1, waiting for transfers between devices, local(): rows = lax.all_gather(panel_rows, 'col', axis=0, tiled=True)  45.2 us
    ppermute x1, waiting for transfers between devices, local(): piece = lax.ppermute(panel_rows, ('row', 'col'), pairs)  23.2 us
    pallas_call x1, Pallas kernels, update(): pl.pallas_call(update_kernel, out_shape=jax.ShapeDtypeStruct((m, n), jnp....  22.1 us
    pallas_call x1, Pallas kernels, apply_inverse(): pl.pallas_call(apply_kernel, out_shape=(jax.ShapeDtypeStruct(own.shape, f...  18.8 us
  transfers between devices with their start and end apart: 3, of which 2 were waited for; matrix products, arithmetic and copies ran while one was open for 0% of the time, Pallas kernels for 43%

profile of v1, /device:TPU:37, one launch (start us, length us, event | category | flops | bytes accessed | tf_op | source)
XLA Modules:
  0.0 194.3 jit_solution(15737432902541396711)
XLA Ops:
  7.2 0.0 copy-start.1
  7.2 0.0 all-gather.3.cloned.1.call-start
  7.2 3.8 %collective-permute-start = (f32[128,1024]{1,0:T(8,128)}, f32[128,1024]{1,0:T(8,128)S(1)}, u32[]{:S(2)}, u32[]{:S(2)}) collective-permute-start(f32[128,1024]{1,0:T(8,128)} %own_ref.1), channel_id=1, source_target_pairs={{0,0},{1,16},{2,32},{3,48},{4,64},{5,80},{6,96},{7,112},{8,1},{9,1... | collective-permute-start | bytes 1572872 | tf_op jit(solution)/shard_map/ppermute | solution.py:192
  11.0 23.2 %collective-permute-done = f32[128,1024]{1,0:T(8,128)S(1)} collective-permute-done((f32[128,1024]{1,0:T(8,128)}, f32[128,1024]{1,0:T(8,128)S(1)}, u32[]{:S(2)}, u32[]{:S(2)}) %collective-permute-start) | collective-permute-done | bytes 524320 | tf_op jit(solution)/shard_map/ppermute | solution.py:192
  34.1 0.0 copy-start
  34.2 0.8 copy-done
  34.9 0.0 all-gather.3.cloned.1.call-update
  35.0 0.0 all-gather.5.cloned.1.call-start
  35.0 0.7 all-gather.5.cloned.1.call-update
  35.7 64.9 %factor.1 = (f32[1024,1024]{1,0:T(8,128)}, f32[1024,1024]{1,0:T(8,128)}) custom-call(f32[1024,1024]{1,0:T(8,128)} %a_ref.1), custom_call_target="tpu_custom_call" | custom-call | tf_op jit(solution)/shard_map/factor/pallas_call | solution.py:88
  100.6 0.0 copy-done.1
  100.7 0.1 compare_select_fusion
  100.7 0.1 copy.8
  100.8 0.7 reshape.17.keep_ref
  101.5 0.0 all-gather.3.cloned.1.call-done.c_ref
  101.5 18.8 %apply.1 = (f32[128,1024]{1,0:T(8,128)}, bf16[1024,1024]{1,0:T(8,128)(2,1)}, bf16[1024,1024]{1,0:T(8,128)(2,1)}) custom-call(f32[1024,1024]{1,0:T(8,128)} %get-tuple-element.9.w_ref, f32[128,1024]{1,0:T(8,128)} %own_ref.1, f32[1024,1024]{1,0:T(8,128)} %all-gather.3.cloned.1.call-done.c_ref), custom_call_target="tpu_custom_call" | custom-call | tf_op jit(solution)/shard_map/apply/pallas_call | solution.py:132
  120.3 45.2 %all-gather.5.cloned.1.call-done.r_ref = f32[2048,1024]{1,0:T(8,128)} async-done(((f32[128,1024]{1,0:T(8,128)}), f32[2048,1024]{1,0:T(8,128)}) %all-gather.5.cloned.1.call-update) | async-done | bytes 8388624 | tf_op jit(solution)/shard_map/all_gather | solution.py:191
  165.4 22.1 %update.1 = f32[2048,1024]{1,0:T(8,128)} custom-call(s32[32]{0:T(128)} %reshape.17.keep_ref, f32[2048,1024]{1,0:T(8,128)} %all-gather.5.cloned.1.call-done.r_ref, bf16[1024,1024]{1,0:T(8,128)(2,1)} %get-tuple-element.11.yh_ref, bf16[1024,1024]{1,0:T(8,128)(2,1)} %get-tuple-element.12.yl_ref, f32[2048,1024]{1,0:T(8,128)} %t_ref.1), custom_call_target="tpu_custom_call" | custom-call | tf_op jit(solution)/shard_map/update/pallas_call | solution.py:164
  (2 shorter events, 0.0 us)
Async XLA Ops:
  7.2 93.5 %copy-start.1 = (s32[8,4]{0,1:T(4,128)S(1)}, s32[8,4]{0,1:T(4,128)}, u32[]{:S(2)}) copy-start(s32[8,4]{0,1:T(4,128)} %param.7) | copy-start | bytes 388
  7.2 94.3 %all-gather.3.cloned.1.call-start = ((), (), s32[]{:S(2)}) async-start(), calls=%async_computation | async-start | bytes 4718592 | tf_op jit(solution)/shard_map/all_gather | solution.py:193
  7.2 26.9 %collective-permute-start = (f32[128,1024]{1,0:T(8,128)}, f32[128,1024]{1,0:T(8,128)S(1)}, u32[]{:S(2)}, u32[]{:S(2)}) collective-permute-start(f32[128,1024]{1,0:T(8,128)} %own_ref.1), channel_id=1, source_target_pairs={{0,0},{1,16},{2,32},{3,48},{4,64},{5,80},{6,96},{7,112},{8,1},{9,1... | collective-permute-start | bytes 1572872 | tf_op jit(solution)/shard_map/ppermute | solution.py:192
  34.1 0.8 copy-start
  35.0 130.5 %all-gather.5.cloned.1.call-start = ((), (), s32[]{:S(2)}) async-start(), calls=%async_computation.1 | async-start | bytes 8912896 | tf_op jit(solution)/shard_map/all_gather | solution.py:191
Sparse Core Ops, SparseCore 0:
  35.1 56.9 all-gather.2
  94.2 71.1 all-gather.4

commit v2 on v1

--- a/solution.py
+++ b/solution.py
@@ -6,7 +6,23 @@
 from jax.sharding import PartitionSpec as P
 
 BLOCK = 256
+SIDE = 4
 HI = lax.Precision.HIGHEST
+MESH = pl.DeviceIdType.MESH
+
+NT = (((1,), (1,)), ((), ()))
+NN = (((1,), (0,)), ((), ()))
+
+
+def halves(x):
+    high = x.astype(jnp.bfloat16)
+    return high, (x - high.astype(jnp.float32)).astype(jnp.bfloat16)
+
+
+def dot3(a, b, dims):
+    def one(x, y):
+        return lax.dot_general(x, y, dims, preferred_element_type=jnp.float32)
+    return one(a[0], b[0]) + (one(a[0], b[1]) + one(a[1], b[0]))
 
 
 def factor_tile(s, t):
@@ -47,9 +63,221 @@
         s[g], t[g] = u, w
     return s, t
 
-def chol_kernel(a_ref, l_ref, w_ref, g_ref, u_ref, wd_ref):
+
+class Exchange:
+    def __init__(self, own, rows, cols, sems):
+        self.own, self.rows, self.cols = own, rows, cols
+        self.row_send, self.row_recv, self.col_send, self.col_recv, self.pair_send, self.here = sems
+        row, col = lax.axis_index("row"), lax.axis_index("col")
+        self.z, self.k, self.y, self.x = row // 2, row % 2, col // SIDE, col % SIDE
+        self.piece = own.shape[0]
+        self.half = self.piece // 2
+        self.quarter = self.piece // 4
+
+    def device(self, dx=0, dy=0, dz=0, dk=0):
+        z, k = lax.rem(self.z + dz + SIDE, SIDE), lax.rem(self.k + dk, 2)
+        y, x = lax.rem(self.y + dy + SIDE, SIDE), lax.rem(self.x + dx + SIDE, SIDE)
+        return (z * 2 + k, y * SIDE + x)
+
+    def greet(self):
+        near = [self.device(dx=1), self.device(dx=-1), self.device(dy=1), self.device(dy=-1),
+                self.device(dz=1), self.device(dz=-1), self.device(dk=1)]
+        barrier = pltpu.get_barrier_semaphore()
+        for device in near:
+            pl.semaphore_signal(barrier, inc=1, device_id=device, device_id_type=MESH)
+        pl.semaphore_wait(barrier, len(near))
+
+    def origin(self, h, a, b):
+        dx, dy = (a, b) if h == 0 else (b, a)
+        return lax.rem(self.x + dx, SIDE), lax.rem(self.y + dy, SIDE)
+
+    def row_slot(self, h, a, b, q=None):
+        x, y = self.origin(h, a, b)
+        start = (y * SIDE + x) * self.piece + h * self.half
+        if q is None:
+            return self.rows.at[pl.ds(pl.multiple_of(start, self.quarter), self.half)]
+        return self.rows.at[pl.ds(pl.multiple_of(start + q * self.quarter, self.quarter), self.quarter)]
+
+    def own_half(self, h):
+        return self.own.at[pl.ds(h * self.half, self.half)]
+
+    def row_copy(self, h, a, b, q, along, sign):
+        to_a = (a - sign) % SIDE if along == 0 else a
+        to_b = (b - sign) % SIDE if along == 1 else b
+        index = ((h * SIDE + to_a) * SIDE + to_b) * 2 + (q or 0)
+        slot = self.row_slot(h, a, b, q)
+        src = self.own_half(h) if (a, b) == (0, 0) else slot
+        on_x = (along == 0) == (h == 0)
+        device = self.device(dx=sign) if on_x else self.device(dy=sign)
+        return pltpu.make_async_remote_copy(
+            src_ref=src, dst_ref=slot, send_sem=self.row_send.at[index], recv_sem=self.row_recv.at[index],
+            device_id=device, device_id_type=MESH)
+
+    def row_wait(self, h, a, b, q=None):
+        index = ((h * SIDE + a) * SIDE + b) * 2 + (q or 0)
+        slot = self.row_slot(h, a, b, q)
+        pltpu.make_async_copy(slot, slot, self.row_recv.at[index]).wait()
+
+    def sends(self):
+        out = []
+        for h in (0, 1):
+            for sign in (1, -1):
+                out.append((0, h, 0, 0, None, 0, sign))
+        for h in (0, 1):
+            for sign in (1, -1):
+                out.append((0, h, 0, 0, None, 1, sign))
+        for h in (0, 1):
+            out += [(1, h, 3, 0, 0, 0, 1), (1, h, 1, 0, 1, 0, -1)]
+        for h in (0, 1):
+            for a in (1, 3):
+                for sign in (1, -1):
+                    out.append((1, h, a, 0, None, 1, sign))
+        for h in (0, 1):
+            for sign in (1, -1):
+                out.append((2, h, 2, 0, None, 1, sign))
+        for wave, places in ((2, (0,)), (3, (1, 3)), (4, (2,))):
+            for h in (0, 1):
+                for a in places:
+                    out += [(wave, h, a, 3, 0, 1, 1), (wave, h, a, 1, 1, 1, -1)]
+        return out
+
+    ARRIVALS = (
+        (),
+        ((1, 0), (3, 0)),
+        ((2, 0), (0, 1), (0, 3)),
+        ((1, 1), (1, 3), (3, 1), (3, 3)),
+        ((2, 1), (2, 3), (0, 2)),
+        ((1, 2), (3, 2), (2, 2)),
+    )
+
+    def col_slot(self, h, a, b):
+        x, y = self.origin(h, a, b)
+        start = (lax.rem(y, 2) * SIDE + x) * self.piece + h * self.half
+        return self.cols.at[pl.ds(pl.multiple_of(start, self.half), self.half)]
+
+    def col_index(self, h, a, b):
+        return (h * SIDE + a) * SIDE + b
+
+    def in_cols(self, h, a, b):
+        _, y = self.origin(h, a, b)
+        return y // 2 == lax.rem(self.x, 2)
+
+    def holder(self):
+        return self.k == self.x // 2
+
+    def hop(self, h):
+        return lax.rem(self.z - self.y + SIDE, SIDE) if h == 0 else lax.rem(self.y - self.z + SIDE, SIDE)
+
+    def col_source(self, h, a, b, first):
+        if not first:
+            return self.col_slot(h, a, b)
+        return self.own_half(h) if (a, b) == (0, 0) else self.row_slot(h, a, b)
+
+    def along(self, h, a, b, first):
+        index = self.col_index(h, a, b)
+        return pltpu.make_async_remote_copy(
+            src_ref=self.col_source(h, a, b, first), dst_ref=self.col_slot(h, a, b),
+            send_sem=self.col_send.at[index], recv_sem=self.col_recv.at[index],
+            device_id=self.device(dz=1 if h == 0 else -1), device_id_type=MESH)
+
+    def across(self, h, a, b, first):
+        index = self.col_index(h, a, b)
+        return pltpu.make_async_remote_copy(
+            src_ref=self.col_source(h, a, b, first), dst_ref=self.col_slot(h, a, b),
+            send_sem=self.pair_send.at[index], recv_sem=self.col_recv.at[index],
+            device_id=self.device(dk=1), device_id_type=MESH)
+
+    def keep_copy(self, h, a, b):
+        src = self.col_source(h, a, b, True)
+        return pltpu.make_async_copy(src, self.col_slot(h, a, b), self.here.at[self.col_index(h, a, b)])
+
+    def col_wait(self, h, a, b):
+        slot = self.col_slot(h, a, b)
+        pltpu.make_async_copy(slot, slot, self.col_recv.at[self.col_index(h, a, b)]).wait()
+
+    def pieces(self, wave):
+        return [(h, a, b) for h in (0, 1) for a, b in (((0, 0),) if wave == 0 else self.ARRIVALS[wave])]
+
+    def start_rows(self, wave):
+        for h in (0, 1):
+            for a, b in self.ARRIVALS[wave]:
+                if b == 2 or (a == 2 and b == 0):
+                    self.row_wait(h, a, b, 0)
+                    self.row_wait(h, a, b, 1)
+                else:
+                    self.row_wait(h, a, b)
+        for entry in self.sends():
+            if entry[0] == wave:
+                self.row_copy(*entry[1:]).start()
+
+    def start_cols(self, wave):
+        for h, a, b in self.pieces(wave):
+            @pl.when(self.in_cols(h, a, b) & self.holder() & (self.hop(h) == 0))
+            def _():
+                self.along(h, a, b, True).start()
+                self.across(h, a, b, True).start()
+                self.keep_copy(h, a, b).start()
+
+    def relay_cols(self, wave, hop):
+        for h, a, b in self.pieces(wave):
+            @pl.when(self.in_cols(h, a, b) & self.holder() & (self.hop(h) == hop))
+            def _():
+                self.col_wait(h, a, b)
+                if hop < SIDE - 1:
+                    self.along(h, a, b, False).start()
+                self.across(h, a, b, False).start()
+
+    def finish_cols(self):
+        for wave in range(len(self.ARRIVALS)):
+            for h, a, b in self.pieces(wave):
+                inside = self.in_cols(h, a, b)
+
+                @pl.when(inside & self.holder() & (self.hop(h) == 0))
+                def _():
+                    self.keep_copy(h, a, b).wait()
+
+                @pl.when(inside & jnp.logical_not(self.holder()))
+                def _():
+                    self.col_wait(h, a, b)
+
+    def finish(self):
+        for entry in self.sends():
+            self.row_copy(*entry[1:]).wait_send()
+        for wave in range(len(self.ARRIVALS)):
+            for h, a, b in self.pieces(wave):
+                @pl.when(self.in_cols(h, a, b) & self.holder())
+                def _():
+                    self.across(h, a, b, False).wait_send()
+
+                    @pl.when(self.hop(h) < SIDE - 1)
+                    def _():
+                        self.along(h, a, b, False).wait_send()
+
+
+ROW_POINTS = (0, 2, 4, 7, 9, 11)
+LAG = 1
+
+
+def transfers(exchange, point):
+    for wave, at in enumerate(ROW_POINTS):
+        if at == point:
+            exchange.start_rows(wave)
+            exchange.start_cols(wave)
+        for hop in range(1, SIDE):
+            if at + LAG * hop == point:
+                exchange.relay_cols(wave, hop)
+
+
+def factor_kernel(a_ref, own_ref, l_ref, x_ref, yh_ref, yl_ref, rows_ref,
+                  w_ref, g_ref, u_ref, wd_ref, cols_ref, wh, wl, ch, cl, zh, zl, sem_own, *sems):
     n = a_ref.shape[0]
     nb = n // 128
+    exchange = Exchange(own_ref, rows_ref, cols_ref, sems)
+    exchange.greet()
+    first = pl.multiple_of(lax.axis_index("col") * own_ref.shape[0], own_ref.shape[0])
+    keep_own = pltpu.make_async_copy(own_ref, rows_ref.at[pl.ds(first, own_ref.shape[0])], sem_own)
+    keep_own.start()
+    transfers(exchange, 0)
     w_ref[...] = a_ref[...]
     l_ref[...] = jnp.zeros_like(l_ref)
     sub = lax.broadcasted_iota(jnp.int32, (8, 128), 0)
@@ -64,6 +292,10 @@
         for g in range(16):
             u_ref[8 * g:8 * g + 8, :] = jnp.where(lane >= sub + 8 * g, s[g], 0.0)
             wd_ref[8 * g:8 * g + 8, :] = t[g]
+        for k in range(nb):
+            @pl.when(p == k)
+            def _():
+                transfers(exchange, 2 * k + 1)
         wd = wd_ref[...]
         rows = w_ref[pl.ds(o, 128), :]
         g_ref[...] = jnp.dot(wd, rows, precision=HI, preferred_element_type=jnp.float32)
@@ -79,42 +311,17 @@
             w_ref[pl.ds(oi, 128), :] -= jnp.dot(li, g_ref[...], precision=HI, preferred_element_type=jnp.float32)
             return c
         lax.fori_loop(p + 1, nb, below, 0)
+        for k in range(nb):
+            @pl.when(p == k)
+            def _():
+                transfers(exchange, 2 * k + 2)
         return carry
     lax.fori_loop(0, nb, panel, 0)
 
-def chol(a):
-    n = a.shape[0]
-    f32 = jnp.float32
-    return pl.pallas_call(
-        chol_kernel,
-        out_shape=(jax.ShapeDtypeStruct((n, n), f32),) * 2,
-        in_specs=[pl.BlockSpec(memory_space=pltpu.VMEM)],
-        out_specs=(pl.BlockSpec(memory_space=pltpu.VMEM),) * 2,
-        scratch_shapes=[pltpu.VMEM((128, n), f32), pltpu.VMEM((128, 128), f32), pltpu.VMEM((128, 128), f32)],
-        compiler_params=pltpu.CompilerParams(vmem_limit_bytes=60 << 20),
-        name="factor",
-    )(a)
-
-NT = (((1,), (1,)), ((), ()))
-NN = (((1,), (0,)), ((), ()))
-
-
-def halves(x):
-    high = x.astype(jnp.bfloat16)
-    return high, (x - high.astype(jnp.float32)).astype(jnp.bfloat16)
-
-
-def dot3(a, b, dims):
-    def one(x, y):
-        return lax.dot_general(x, y, dims, preferred_element_type=jnp.float32)
-    return one(a[0], b[0]) + (one(a[0], b[1]) + one(a[1], b[0]))
-
-
-def apply_kernel(w_ref, own_ref, c_ref, x_ref, yh_ref, yl_ref, wh, wl, ch, cl, zh, zl):
-    n = w_ref.shape[0]
+    x_ref[...] = lax.dot_general(own_ref[...], w_ref[...], NT, precision=HI, preferred_element_type=jnp.float32)
     wh[...], wl[...] = halves(w_ref[...])
-    ch[...], cl[...] = halves(c_ref[...])
-    x_ref[...] = lax.dot_general(own_ref[...], w_ref[...], NT, precision=HI, preferred_element_type=jnp.float32)
+    exchange.finish_cols()
+    ch[...], cl[...] = halves(cols_ref[...])
     for p in range(0, n, BLOCK):
         e = p + BLOCK
         z = dot3((ch[:, :e], cl[:, :e]), (wh[p:e, :e], wl[p:e, :e]), NT)
@@ -123,22 +330,37 @@
         e = p + BLOCK
         y = dot3((zh[:, p:], zl[:, p:]), (wh[p:, p:e], wl[p:, p:e]), NN)
         yh_ref[:, p:e], yl_ref[:, p:e] = halves(y)
-
-
-def apply_inverse(w, own, c):
+    exchange.finish()
+    keep_own.wait()
+
+
+def factor(front_diag, own, cols):
     f32, bf = jnp.float32, jnp.bfloat16
-    n, m = w.shape[0], c.shape[0]
-    vm = pl.BlockSpec(memory_space=pltpu.VMEM)
+    n = front_diag.shape[0]
+    pieces = lax.axis_size("col")
+    vm, anywhere = pl.BlockSpec(memory_space=pltpu.VMEM), pl.BlockSpec(memory_space=pl.ANY)
+    dma = pltpu.SemaphoreType.DMA
     return pl.pallas_call(
-        apply_kernel,
-        out_shape=(jax.ShapeDtypeStruct(own.shape, f32), jax.ShapeDtypeStruct((m, n), bf), jax.ShapeDtypeStruct((m, n), bf)),
-        in_specs=[vm] * 3,
-        out_specs=(vm,) * 3,
-        scratch_shapes=[pltpu.VMEM((n, n), bf)] * 2 + [pltpu.VMEM((m, n), bf)] * 4,
-        compiler_params=pltpu.CompilerParams(vmem_limit_bytes=60 << 20),
-        name="apply",
-    )(w, own, c)
-
+        factor_kernel,
+        out_shape=(
+            jax.ShapeDtypeStruct((n, n), f32),
+            jax.ShapeDtypeStruct(own.shape, f32),
+            jax.ShapeDtypeStruct((cols, n), bf),
+            jax.ShapeDtypeStruct((cols, n), bf),
+            jax.ShapeDtypeStruct((pieces * own.shape[0], n), f32),
+        ),
+        in_specs=[vm, vm],
+        out_specs=(vm, vm, vm, vm, anywhere),
+        scratch_shapes=[
+            pltpu.VMEM((n, n), f32), pltpu.VMEM((128, n), f32), pltpu.VMEM((128, 128), f32), pltpu.VMEM((128, 128), f32),
+            pltpu.VMEM((cols, n), f32),
+            pltpu.VMEM((n, n), bf), pltpu.VMEM((n, n), bf),
+            pltpu.VMEM((cols, n), bf), pltpu.VMEM((cols, n), bf), pltpu.VMEM((cols, n), bf), pltpu.VMEM((cols, n), bf),
+            dma, dma((64,)), dma((64,)), dma((32,)), dma((32,)), dma((32,)), dma((32,)),
+        ],
+        compiler_params=pltpu.CompilerParams(vmem_limit_bytes=60 << 20, collective_id=0, has_side_effects=True),
+        name="factor",
+    )(front_diag, own)
 
 def update_kernel(keep_ref, r_ref, yh_ref, yl_ref, t_ref, o_ref, rh, rl):
     i = pl.program_id(0)
@@ -182,17 +404,7 @@
 
 
 def local(front_diag, panel_rows, trailing, pattern):
-    nrow, ncol = lax.axis_size("row"), lax.axis_size("col")
-    ratio = ncol // nrow
-    pairs = []
-    for c in range(ncol):
-        for r in range(nrow):
-            pairs.append(((c // ratio) * ncol + (c % ratio) * nrow + r, r * ncol + c))
-    rows = lax.all_gather(panel_rows, "col", axis=0, tiled=True)
-    piece = lax.ppermute(panel_rows, ("row", "col"), pairs)
-    col_rows = lax.all_gather(piece, "row", axis=0, tiled=True)
-    diag_factor, inverse = chol(front_diag)
-    panel_factor, yh, yl = apply_inverse(inverse, panel_rows, col_rows)
+    diag_factor, panel_factor, yh, yl, rows = factor(front_diag, panel_rows, trailing.shape[1])
     row_blocks, col_blocks = pattern.shape
     row_index = lax.axis_index("row") * row_blocks + jnp.arange(row_blocks)
     col_index = lax.axis_index("col") * col_blocks + jnp.arange(col_blocks)

time: 195 us -> 153 us (0.78)
  the two profiles are of different devices: /device:TPU:37 before, /device:TPU:112 now
where the time goes in v2:
time: 153 us
  Pallas kernels  145 us (95%)
  local copies, waits for them, and re-layouts  6.32 us (4%)
    pallas_call x1, Pallas kernels, factor(): pl.pallas_call(factor_kernel, out_shape=(jax.ShapeDtypeStruct((n, n), f32...  127 us
    pallas_call x1, Pallas kernels, update(): pl.pallas_call(update_kernel, out_shape=jax.ShapeDtypeStruct((m, n), jnp....  18.1 us
    unnamed x4, local copies, waits for them, and re-layouts  5.64 us

profile of v2, /device:TPU:112, one launch (start us, length us, event | category | flops | bytes accessed | tf_op | source)
XLA Modules:
  0.0 152.9 jit_solution(15263287931744863834)
XLA Ops:
  0.7 0.8 compare_select_fusion
  1.4 0.1 copy.8
  1.5 0.6 reshape.17.keep_ref
  2.1 127.1 %factor.1 = (f32[1024,1024]{1,0:T(8,128)}, f32[128,1024]{1,0:T(8,128)}, bf16[1024,1024]{1,0:T(8,128)(2,1)}, bf16[1024,1024]{1,0:T(8,128)(2,1)}, f32[2048,1024]{1,0:T(8,128)}) custom-call(f32[1024,1024]{1,0:T(8,128)} %a_ref.1, f32[128,1024]{1,0:T(8,128)} %own_ref.1), custom_call_target="tpu_custom_call" | custom-call | tf_op jit(solution)/shard_map/factor/pallas_call | solution.py:343
  129.2 18.1 %update.1 = f32[2048,1024]{1,0:T(8,128)} custom-call(s32[32]{0:T(128)} %reshape.17.keep_ref, f32[2048,1024]{1,0:T(8,128)} %get-tuple-element.10.r_ref, bf16[1024,1024]{1,0:T(8,128)(2,1)} %get-tuple-element.11.yh_ref, bf16[1024,1024]{1,0:T(8,128)(2,1)} %get-tuple-element.12.yl_ref, f32[2048,1024]{1,0:T(8,128)} %t_ref.1), custom_call_target="tpu_custom_call" | custom-call | tf_op jit(solution)/shard_map/update/pallas_call | solution.py:386
  147.3 0.0 copy-start
  147.3 4.8 %copy.11 = f32[1024,1024]{1,0:T(8,128)} copy(f32[1024,1024]{1,0:T(8,128)} %get-tuple-element.16) | data formatting | bytes 8388608
  152.1 0.0 copy-done
  152.1 0.8 copy.12
  (2 shorter events, 0.0 us)
Async XLA Ops:
  147.3 4.8 %copy-start = (f32[128,1024]{1,0:T(8,128)S(1)}, f32[128,1024]{1,0:T(8,128)}, u32[]{:S(2)}) copy-start(f32[128,1024]{1,0:T(8,128)} %get-tuple-element.17) | copy-start | bytes 1572868

commit v3 on v2

--- a/solution.py
+++ b/solution.py
@@ -7,6 +7,7 @@
 
 BLOCK = 256
 SIDE = 4
+GROUP = 512
 HI = lax.Precision.HIGHEST
 MESH = pl.DeviceIdType.MESH
 
@@ -64,6 +65,25 @@
     return s, t
 
 
+def thirds(x):
+    f32 = jnp.float32
+    h = x.astype(jnp.bfloat16)
+    r = x - h.astype(f32)
+    m = r.astype(jnp.bfloat16)
+    return h, m, (r - m.astype(f32)).astype(jnp.bfloat16)
+
+def wide_left(x):
+    h, m, l = thirds(x)
+    return jnp.concatenate([h, h, m, m, h, l], axis=1)
+
+def tall_right(x):
+    h, m, l = thirds(x)
+    return jnp.concatenate([h, m, h, m, l, h], axis=0)
+
+def dot6(a, b):
+    return jnp.dot(a, b, preferred_element_type=jnp.float32)
+
+
 class Exchange:
     def __init__(self, own, rows, cols, sems):
         self.own, self.rows, self.cols = own, rows, cols
@@ -165,8 +185,18 @@
     def holder(self):
         return self.k == self.x // 2
 
-    def hop(self, h):
-        return lax.rem(self.z - self.y + SIDE, SIDE) if h == 0 else lax.rem(self.y - self.z + SIDE, SIDE)
+    def at_hop(self, h, hop):
+        if h == 0:
+            return self.z - self.y == hop
+        return (lax.rem(self.y - self.z + SIDE, SIDE) == hop) & (self.y < SIDE - 1)
+
+    def goes_on(self, h):
+        if h == 0:
+            return (self.z >= self.y) & (self.z < SIDE - 1)
+        return (lax.rem(self.y - self.z + SIDE, SIDE) < SIDE - 1) & (self.y < SIDE - 1)
+
+    def needed(self):
+        return self.z >= self.y
 
     def col_source(self, h, a, b, first):
         if not first:
@@ -212,27 +242,38 @@
 
     def start_cols(self, wave):
         for h, a, b in self.pieces(wave):
-            @pl.when(self.in_cols(h, a, b) & self.holder() & (self.hop(h) == 0))
+            inside = self.in_cols(h, a, b) & self.holder() & (self.z == self.y)
+
+            @pl.when(inside)
+            def _():
+                self.across(h, a, b, True).start()
+                self.keep_copy(h, a, b).start()
+
+            @pl.when(inside & (self.z < SIDE - 1))
             def _():
                 self.along(h, a, b, True).start()
-                self.across(h, a, b, True).start()
-                self.keep_copy(h, a, b).start()
-
-    def relay_cols(self, wave, hop):
-        for h, a, b in self.pieces(wave):
-            @pl.when(self.in_cols(h, a, b) & self.holder() & (self.hop(h) == hop))
-            def _():
-                self.col_wait(h, a, b)
-                if hop < SIDE - 1:
-                    self.along(h, a, b, False).start()
-                self.across(h, a, b, False).start()
+
+    def relay_cols(self, h, a, b, hop):
+        here = self.in_cols(h, a, b) & self.holder() & self.at_hop(h, hop)
+
+        @pl.when(here)
+        def _():
+            self.col_wait(h, a, b)
+
+        @pl.when(here & self.goes_on(h))
+        def _():
+            self.along(h, a, b, False).start()
+
+        @pl.when(here & self.needed())
+        def _():
+            self.across(h, a, b, False).start()
 
     def finish_cols(self):
         for wave in range(len(self.ARRIVALS)):
             for h, a, b in self.pieces(wave):
-                inside = self.in_cols(h, a, b)
-
-                @pl.when(inside & self.holder() & (self.hop(h) == 0))
+                inside = self.in_cols(h, a, b) & self.needed()
+
+                @pl.when(inside & self.holder() & (self.z == self.y))
                 def _():
                     self.keep_copy(h, a, b).wait()
 
@@ -245,17 +286,41 @@
             self.row_copy(*entry[1:]).wait_send()
         for wave in range(len(self.ARRIVALS)):
             for h, a, b in self.pieces(wave):
-                @pl.when(self.in_cols(h, a, b) & self.holder())
+                inside = self.in_cols(h, a, b) & self.holder()
+
+                @pl.when(inside & self.needed())
                 def _():
                     self.across(h, a, b, False).wait_send()
 
-                    @pl.when(self.hop(h) < SIDE - 1)
-                    def _():
-                        self.along(h, a, b, False).wait_send()
-
-
-ROW_POINTS = (0, 2, 4, 7, 9, 11)
-LAG = 1
+                @pl.when(inside & self.goes_on(h))
+                def _():
+                    self.along(h, a, b, False).wait_send()
+
+
+ROW_POINTS = (0, 1, 3, 5, 6, 8)
+POINTS = [0.0] + [2.5 + 5.6 * (k + 1) for k in range(8)] + [48.5 + 0.65 * i for i in range(33)]
+
+
+def relay_points():
+    table = {}
+    for kind in ((0, 1), (2, 3), (3, 0), (1, 2)):
+        for h in (0, 1):
+            free = [0.0] * (SIDE - 1)
+            for wave, places in enumerate(Exchange.ARRIVALS):
+                for a, b in (((0, 0),) if wave == 0 else places):
+                    if (b if h == 0 else a) not in kind:
+                        continue
+                    ready = POINTS[ROW_POINTS[wave]]
+                    for hop in range(1, SIDE):
+                        free[hop - 1] = max(ready, free[hop - 1]) + 2.8
+                        arrival = free[hop - 1] + 1.8
+                        point = min([i for i, t in enumerate(POINTS) if t >= arrival], default=len(POINTS) - 1)
+                        ready = POINTS[point]
+                        table[h, a, b, hop] = max(point, table.get((h, a, b, hop), 0))
+    return table
+
+
+RELAYS = relay_points()
 
 
 def transfers(exchange, point):
@@ -263,81 +328,144 @@
         if at == point:
             exchange.start_rows(wave)
             exchange.start_cols(wave)
-        for hop in range(1, SIDE):
-            if at + LAG * hop == point:
-                exchange.relay_cols(wave, hop)
-
-
-def factor_kernel(a_ref, own_ref, l_ref, x_ref, yh_ref, yl_ref, rows_ref,
-                  w_ref, g_ref, u_ref, wd_ref, cols_ref, wh, wl, ch, cl, zh, zl, sem_own, *sems):
+    for (h, a, b, hop), at in RELAYS.items():
+        if at == point:
+            exchange.relay_cols(h, a, b, hop)
+
+
+def factor_kernel(a_ref, own_ref, l_ref, x_ref, yh_ref, yl_ref, ch_ref, cl_ref, rows_ref,
+                  w_ref, g_ref, d_ref, u_ref, wd_ref, cols_ref, wh, wl, r_buf, zf, zh, zl, yh_buf, yl_buf,
+                  sem_a, sem_own, sem_in, sem_out, *sems):
     n = a_ref.shape[0]
     nb = n // 128
+    load = pltpu.make_async_copy(a_ref, w_ref, sem_a)
+    load.start()
     exchange = Exchange(own_ref, rows_ref, cols_ref, sems)
+    l_ref[...] = jnp.zeros_like(l_ref)
+    wd_ref[...] = jnp.zeros_like(wd_ref)
+    u_ref[...] = jnp.zeros_like(u_ref)
     exchange.greet()
-    first = pl.multiple_of(lax.axis_index("col") * own_ref.shape[0], own_ref.shape[0])
+    me = lax.axis_index("col")
+    first = pl.multiple_of(me * own_ref.shape[0], own_ref.shape[0])
     keep_own = pltpu.make_async_copy(own_ref, rows_ref.at[pl.ds(first, own_ref.shape[0])], sem_own)
+    transfers(exchange, 0)
     keep_own.start()
-    transfers(exchange, 0)
-    w_ref[...] = a_ref[...]
-    l_ref[...] = jnp.zeros_like(l_ref)
+    load.wait()
+    d_ref[...] = w_ref[:128, :128]
     sub = lax.broadcasted_iota(jnp.int32, (8, 128), 0)
     lane = lax.broadcasted_iota(jnp.int32, (8, 128), 1)
     lane_all = lax.broadcasted_iota(jnp.int32, (128, n), 1)
 
+    def settle(p, last):
+        q = jnp.maximum(p - 1, 0)
+        oq = pl.multiple_of(q * 128, 128)
+        wd = wd_ref[...]
+        row = w_ref[pl.ds(oq, 128), :]
+        g = dot6(wide_left(wd), tall_right(row))
+        inside = (lane_all >= oq) & (lane_all < oq + 128)
+        done = jnp.where(lane_all < oq, g, 0.0)
+        w_ref[pl.ds(oq, 128), :] = done if last else jnp.where(p > 0, done, row)
+        l_ref[pl.ds(oq, 128), pl.ds(oq, 128)] = u_ref[...].T
+        if last:
+            w_ref[pl.ds(oq, 128), pl.ds(oq, 128)] = wd
+            return
+        g_ref[...] = g
+        g_ref[:, pl.ds(oq, 128)] += wd
+        right = tall_right(g_ref[...])
+        for i in range(1, nb):
+            li = jnp.where(q < i, g[:, i * 128:(i + 1) * 128], 0.0).T
+            l_ref[i * 128:(i + 1) * 128, pl.ds(oq, 128)] = jnp.where(q < i, li, l_ref[i * 128:(i + 1) * 128, pl.ds(oq, 128)])
+            w_ref[i * 128:(i + 1) * 128, :] -= dot6(wide_left(li), right)
+        w_ref[pl.ds(oq, 128), pl.ds(oq, 128)] = jnp.where(p > 0, wd, w_ref[pl.ds(oq, 128), pl.ds(oq, 128)])
+
     def panel(p, carry):
         o = pl.multiple_of(p * 128, 128)
-        s = [w_ref[pl.ds(o + 8 * g, 8), pl.ds(o, 128)] for g in range(16)]
+        o1 = pl.multiple_of(jnp.minimum(p + 1, nb - 1) * 128, 128)
+        s = [d_ref[8 * g:8 * g + 8, :] for g in range(16)]
         t = [(lane == sub + 8 * g).astype(jnp.float32) for g in range(16)]
         s, t = factor_tile(s, t)
+        settle(p, False)
         for g in range(16):
             u_ref[8 * g:8 * g + 8, :] = jnp.where(lane >= sub + 8 * g, s[g], 0.0)
             wd_ref[8 * g:8 * g + 8, :] = t[g]
+        un = dot6(wide_left(wd_ref[...]), tall_right(w_ref[pl.ds(o, 128), pl.ds(o1, 128)]))
+        d_ref[...] = w_ref[pl.ds(o1, 128), pl.ds(o1, 128)] - dot6(wide_left(un.T), tall_right(un))
         for k in range(nb):
             @pl.when(p == k)
             def _():
-                transfers(exchange, 2 * k + 1)
-        wd = wd_ref[...]
-        rows = w_ref[pl.ds(o, 128), :]
-        g_ref[...] = jnp.dot(wd, rows, precision=HI, preferred_element_type=jnp.float32)
-        g_ref[:, pl.ds(o, 128)] = wd
-        w_ref[pl.ds(o, 128), :] = jnp.where(lane_all < o + 128, g_ref[...], 0.0)
-        l_ref[pl.ds(o, 128), pl.ds(o, 128)] = u_ref[...].T
-
-        def below(i, c):
-            oi = pl.multiple_of(i * 128, 128)
-            li = g_ref[:, pl.ds(oi, 128)].T
-            l_ref[pl.ds(oi, 128), pl.ds(o, 128)] = li
-            w_ref[pl.ds(oi, 128), pl.ds(o, 128)] = jnp.zeros((128, 128), jnp.float32)
-            w_ref[pl.ds(oi, 128), :] -= jnp.dot(li, g_ref[...], precision=HI, preferred_element_type=jnp.float32)
-            return c
-        lax.fori_loop(p + 1, nb, below, 0)
-        for k in range(nb):
-            @pl.when(p == k)
-            def _():
-                transfers(exchange, 2 * k + 2)
+                transfers(exchange, k + 1)
         return carry
     lax.fori_loop(0, nb, panel, 0)
-
-    x_ref[...] = lax.dot_general(own_ref[...], w_ref[...], NT, precision=HI, preferred_element_type=jnp.float32)
+    keep_own.wait()
+
+    def fetch(b, slot):
+        rows = rows_ref.at[pl.ds(pl.multiple_of(b * GROUP, GROUP), GROUP)]
+        return pltpu.make_async_copy(rows, r_buf.at[slot], sem_in.at[slot])
+
+    def store(b, slot):
+        part = pl.ds(pl.multiple_of(b * GROUP, GROUP), GROUP)
+        return (pltpu.make_async_copy(yh_buf.at[slot], yh_ref.at[part], sem_out.at[slot, 0]),
+                pltpu.make_async_copy(yl_buf.at[slot], yl_ref.at[part], sem_out.at[slot, 1]))
+
+    blocks = rows_ref.shape[0] // GROUP
+    fetch(0, 0).start()
+    settle(nb, True)
     wh[...], wl[...] = halves(w_ref[...])
+
+    def passing(b, j):
+        for k in range(blocks):
+            if any(at == nb + 1 + 8 * k + j for at in RELAYS.values()):
+                @pl.when(b == k)
+                def _():
+                    transfers(exchange, nb + 1 + 8 * k + j)
+
+    def transform(b, carry):
+        slot = lax.rem(b, 2)
+        fetch(b, slot).wait()
+
+        @pl.when(b + 1 < blocks)
+        def _():
+            fetch(b + 1, 1 - slot).start()
+
+        @pl.when(b >= 2)
+        def _():
+            for copy in store(b - 2, slot):
+                copy.wait()
+        rh, rl = halves(r_buf[slot])
+        zh[...], zl[...] = rh, rl
+        for j, p in enumerate(range(0, n, BLOCK)):
+            e = p + BLOCK
+            zf[:, p:e] = dot3((zh[:, :e], zl[:, :e]), (wh[p:e, :e], wl[p:e, :e]), NT)
+            passing(b, j)
+        per = GROUP // own_ref.shape[0]
+
+        @pl.when(me // per == b)
+        def _():
+            x_ref[...] = zf[pl.ds(pl.multiple_of(lax.rem(me, per) * own_ref.shape[0], own_ref.shape[0]), own_ref.shape[0]), :]
+        rh, rl = halves(zf[...])
+        zh[...], zl[...] = rh, rl
+        for j, p in enumerate(range(0, n, BLOCK)):
+            e = p + BLOCK
+            y = dot3((zh[:, p:], zl[:, p:]), (wh[p:, p:e], wl[p:, p:e]), NN)
+            yh_buf[slot, :, p:e], yl_buf[slot, :, p:e] = halves(y)
+            passing(b, 4 + j)
+        for copy in store(b, slot):
+            copy.start()
+        return carry
+    lax.fori_loop(0, blocks, transform, 0)
+    transfers(exchange, len(POINTS) - 1)
     exchange.finish_cols()
-    ch[...], cl[...] = halves(cols_ref[...])
-    for p in range(0, n, BLOCK):
-        e = p + BLOCK
-        z = dot3((ch[:, :e], cl[:, :e]), (wh[p:e, :e], wl[p:e, :e]), NT)
-        zh[:, p:e], zl[:, p:e] = halves(z)
-    for p in range(0, n, BLOCK):
-        e = p + BLOCK
-        y = dot3((zh[:, p:], zl[:, p:]), (wh[p:, p:e], wl[p:, p:e]), NN)
-        yh_ref[:, p:e], yl_ref[:, p:e] = halves(y)
+    ch_ref[...], cl_ref[...] = halves(cols_ref[...])
     exchange.finish()
-    keep_own.wait()
+    for b in (blocks - 2, blocks - 1):
+        for copy in store(b, b % 2):
+            copy.wait()
 
 
 def factor(front_diag, own, cols):
     f32, bf = jnp.float32, jnp.bfloat16
     n = front_diag.shape[0]
-    pieces = lax.axis_size("col")
+    rows = lax.axis_size("col") * own.shape[0]
     vm, anywhere = pl.BlockSpec(memory_space=pltpu.VMEM), pl.BlockSpec(memory_space=pl.ANY)
     dma = pltpu.SemaphoreType.DMA
     return pl.pallas_call(
@@ -345,34 +473,42 @@
         out_shape=(
             jax.ShapeDtypeStruct((n, n), f32),
             jax.ShapeDtypeStruct(own.shape, f32),
+            jax.ShapeDtypeStruct((rows, n), bf),
+            jax.ShapeDtypeStruct((rows, n), bf),
             jax.ShapeDtypeStruct((cols, n), bf),
             jax.ShapeDtypeStruct((cols, n), bf),
-            jax.ShapeDtypeStruct((pieces * own.shape[0], n), f32),
+            jax.ShapeDtypeStruct((rows, n), f32),
         ),
-        in_specs=[vm, vm],
-        out_specs=(vm, vm, vm, vm, anywhere),
+        in_specs=[anywhere, vm],
+        out_specs=(vm, vm, anywhere, anywhere, vm, vm, anywhere),
         scratch_shapes=[
-            pltpu.VMEM((n, n), f32), pltpu.VMEM((128, n), f32), pltpu.VMEM((128, 128), f32), pltpu.VMEM((128, 128), f32),
+            pltpu.VMEM((n, n), f32), pltpu.VMEM((128, n), f32),
+            pltpu.VMEM((128, 128), f32), pltpu.VMEM((128, 128), f32), pltpu.VMEM((128, 128), f32),
             pltpu.VMEM((cols, n), f32),
             pltpu.VMEM((n, n), bf), pltpu.VMEM((n, n), bf),
-            pltpu.VMEM((cols, n), bf), pltpu.VMEM((cols, n), bf), pltpu.VMEM((cols, n), bf), pltpu.VMEM((cols, n), bf),
-            dma, dma((64,)), dma((64,)), dma((32,)), dma((32,)), dma((32,)), dma((32,)),
+            pltpu.VMEM((2, GROUP, n), f32), pltpu.VMEM((GROUP, n), f32),
+            pltpu.VMEM((GROUP, n), bf), pltpu.VMEM((GROUP, n), bf),
+            pltpu.VMEM((2, GROUP, n), bf), pltpu.VMEM((2, GROUP, n), bf),
+            dma, dma, dma((2,)), dma((2, 2)),
+            dma((64,)), dma((64,)), dma((32,)), dma((32,)), dma((32,)), dma((32,)),
         ],
-        compiler_params=pltpu.CompilerParams(vmem_limit_bytes=60 << 20, collective_id=0, has_side_effects=True),
+        compiler_params=pltpu.CompilerParams(vmem_limit_bytes=56 << 20, collective_id=0, has_side_effects=True),
         name="factor",
     )(front_diag, own)
 
-def update_kernel(keep_ref, r_ref, yh_ref, yl_ref, t_ref, o_ref, rh, rl):
+
+def update_kernel(keep_ref, rh_ref, rl_ref, ch_ref, cl_ref, t_ref, l_ref, x_ref, o_ref, lo_ref, xo_ref):
     i = pl.program_id(0)
+    lo_ref[...] = l_ref[...]
+    xo_ref[...] = x_ref[...]
     cols = o_ref.shape[1] // BLOCK
-    rh[...], rl[...] = halves(r_ref[...])
     for j in range(cols):
         part = slice(j * BLOCK, (j + 1) * BLOCK)
         kept = keep_ref[i * cols + j] != 0
 
         @pl.when(kept)
         def _():
-            d = dot3((rh[...], rl[...]), (yh_ref[part, :], yl_ref[part, :]), NT)
+            d = dot3((rh_ref[...], rl_ref[...]), (ch_ref[part, :], cl_ref[part, :]), NT)
             o_ref[:, part] = t_ref[:, part] - d
 
         @pl.when(jnp.logical_not(kept))
@@ -380,36 +516,35 @@
             o_ref[:, part] = t_ref[:, part]
 
 
-def update(keep, rows, yh, yl, trailing):
+def update(keep, rh, rl, ch, cl, trailing, diag_factor, panel_factor):
     m, n = trailing.shape
-    k = rows.shape[1]
+    k = rh.shape[1]
+    steps = m // BLOCK
+    row = lambda size, width: pl.BlockSpec((size, width), lambda i, s: (i, 0))
+    whole = lambda size, width: pl.BlockSpec((size, width), lambda i, s: (0, 0))
+    ld, lx = diag_factor.shape[0] // steps, panel_factor.shape[0] // steps
     return pl.pallas_call(
         update_kernel,
-        out_shape=jax.ShapeDtypeStruct((m, n), jnp.float32),
+        out_shape=(jax.ShapeDtypeStruct((m, n), jnp.float32), jax.ShapeDtypeStruct(diag_factor.shape, jnp.float32),
+                   jax.ShapeDtypeStruct(panel_factor.shape, jnp.float32)),
         grid_spec=pltpu.PrefetchScalarGridSpec(
             num_scalar_prefetch=1,
-            grid=(m // BLOCK,),
-            in_specs=[
-                pl.BlockSpec((BLOCK, k), lambda i, s: (i, 0)),
-                pl.BlockSpec((n, k), lambda i, s: (0, 0)),
-                pl.BlockSpec((n, k), lambda i, s: (0, 0)),
-                pl.BlockSpec((BLOCK, n), lambda i, s: (i, 0)),
-            ],
-            out_specs=pl.BlockSpec((BLOCK, n), lambda i, s: (i, 0)),
-            scratch_shapes=[pltpu.VMEM((BLOCK, k), jnp.bfloat16)] * 2,
+            grid=(steps,),
+            in_specs=[row(BLOCK, k), row(BLOCK, k), whole(n, k), whole(n, k), row(BLOCK, n), row(ld, k), row(lx, k)],
+            out_specs=(row(BLOCK, n), row(ld, k), row(lx, k)),
         ),
         compiler_params=pltpu.CompilerParams(vmem_limit_bytes=60 << 20),
         name="update",
-    )(keep, rows, yh, yl, trailing)
+    )(keep, rh, rl, ch, cl, trailing, diag_factor, panel_factor)
 
 
 def local(front_diag, panel_rows, trailing, pattern):
-    diag_factor, panel_factor, yh, yl, rows = factor(front_diag, panel_rows, trailing.shape[1])
     row_blocks, col_blocks = pattern.shape
     row_index = lax.axis_index("row") * row_blocks + jnp.arange(row_blocks)
     col_index = lax.axis_index("col") * col_blocks + jnp.arange(col_blocks)
     keep = pattern * (row_index[:, None] >= col_index[None, :]).astype(jnp.int32)
-    schur = update(keep.reshape(-1), rows, yh, yl, trailing)
+    diag_factor, panel_factor, yh, yl, ch, cl, _ = factor(front_diag, panel_rows, trailing.shape[1])
+    schur, diag_factor, panel_factor = update(keep.reshape(-1), yh, yl, ch, cl, trailing, diag_factor, panel_factor)
     return (diag_factor, panel_factor, schur)
 
 

time: 153 us -> 121 us (0.79)
  the two profiles are of different devices: /device:TPU:112 before, /device:TPU:34 now
where the time goes in v3:
time: 121 us; the launch traced here: 120 us
  Pallas kernels  118 us (98%)
    pallas_call x1, Pallas kernels, factor(): pl.pallas_call(factor_kernel, out_shape=(jax.ShapeDtypeStruct((n, n), f32...  95 us
    pallas_call x1, Pallas kernels, update(): pl.pallas_call(update_kernel, out_shape=(jax.ShapeDtypeStruct((m, n), jnp...  23.2 us

profile of v3, /device:TPU:34, one launch (start us, length us, event | category | flops | bytes accessed | tf_op | source)
XLA Modules:
  0.0 120.2 jit_solution(10139982875006098137)
XLA Ops:
  0.7 0.8 compare_select_fusion
  1.4 0.1 copy.8
  1.5 0.6 reshape.17.keep_ref
  2.1 95.0 %factor.1 = (f32[1024,1024]{1,0:T(8,128)}, f32[128,1024]{1,0:T(8,128)}, bf16[2048,1024]{1,0:T(8,128)(2,1)}, bf16[2048,1024]{1,0:T(8,128)(2,1)}, bf16[1024,1024]{...) custom-call(f32[1024,1024]{1,0:T(8,128)} %a_ref.1, f32[128,1024]{1,0:T(8,128)} %own_ref.1), custom_call_target="tpu_custom_call" | custom-call | tf_op jit(solution)/shard_map/factor/pallas_call | solution.py:471
  97.0 23.2 %update.1 = (f32[2048,1024]{1,0:T(8,128)}, f32[1024,1024]{1,0:T(8,128)}, f32[128,1024]{1,0:T(8,128)}) custom-call(s32[32]{0:T(128)} %reshape.17.keep_ref, bf16[2048,1024]{1,0:T(8,128)(2,1)} %get-tuple-element.12.rh_ref, bf16[2048,1024]{1,0:T(8,128)(2,1)} %get-tuple-element.13.rl_ref, bf16[1024,1024]{1,0:T(8,128)(2,1)} %get-tuple-element.14.ch_ref, ...), custom_call_target="tpu_custom_call" | custom-call | tf_op jit(solution)/shard_map/update/pallas_call | solution.py:526
  (2 shorter events, 0.0 us)

commit v4 on v3

--- a/solution.py
+++ b/solution.py
@@ -298,7 +298,8 @@
 
 
 ROW_POINTS = (0, 1, 3, 5, 6, 8)
-POINTS = [0.0] + [2.5 + 5.6 * (k + 1) for k in range(8)] + [48.5 + 0.65 * i for i in range(33)]
+STEPS = 4
+POINTS = [0.0] + [2.5 + 5.6 * (k + 1) for k in range(8)] + [49.5 + 0.65 * i for i in range(16)] + [60.5 + 0.7 * i for i in range(40)]
 
 
 def relay_points():
@@ -333,11 +334,13 @@
             exchange.relay_cols(h, a, b, hop)
 
 
-def factor_kernel(a_ref, own_ref, l_ref, x_ref, yh_ref, yl_ref, ch_ref, cl_ref, rows_ref,
-                  w_ref, g_ref, d_ref, u_ref, wd_ref, cols_ref, wh, wl, r_buf, zf, zh, zl, yh_buf, yl_buf,
-                  sem_a, sem_own, sem_in, sem_out, *sems):
+def factor_kernel(a_ref, own_in, l_out, x_ref, yh_ref, yl_ref, zh_ref, zl_ref, rows_ref,
+                  w_ref, l_ref, g_ref, d_ref, u_ref, wd_ref, cols_ref, wh, wl, r_buf, zf, rh, rl, yh_buf, yl_buf,
+                  ch, cl, zh_buf, zl_buf, own_ref, sem_a, sem_own, sem_l, sem_in, sem_out, sem_z, *sems):
     n = a_ref.shape[0]
     nb = n // 128
+    load_own = pltpu.make_async_copy(own_in, own_ref, sem_own)
+    load_own.start()
     load = pltpu.make_async_copy(a_ref, w_ref, sem_a)
     load.start()
     exchange = Exchange(own_ref, rows_ref, cols_ref, sems)
@@ -345,6 +348,7 @@
     wd_ref[...] = jnp.zeros_like(wd_ref)
     u_ref[...] = jnp.zeros_like(u_ref)
     exchange.greet()
+    load_own.wait()
     me = lax.axis_index("col")
     first = pl.multiple_of(me * own_ref.shape[0], own_ref.shape[0])
     keep_own = pltpu.make_async_copy(own_ref, rows_ref.at[pl.ds(first, own_ref.shape[0])], sem_own)
@@ -410,14 +414,17 @@
     blocks = rows_ref.shape[0] // GROUP
     fetch(0, 0).start()
     settle(nb, True)
+    save_l = pltpu.make_async_copy(l_ref, l_out, sem_l)
+    save_l.start()
     wh[...], wl[...] = halves(w_ref[...])
 
     def passing(b, j):
         for k in range(blocks):
-            if any(at == nb + 1 + 8 * k + j for at in RELAYS.values()):
+            at = nb + 1 + STEPS * k + j
+            if at in RELAYS.values():
                 @pl.when(b == k)
                 def _():
-                    transfers(exchange, nb + 1 + 8 * k + j)
+                    transfers(exchange, at)
 
     def transform(b, carry):
         slot = lax.rem(b, 2)
@@ -431,35 +438,41 @@
         def _():
             for copy in store(b - 2, slot):
                 copy.wait()
-        rh, rl = halves(r_buf[slot])
-        zh[...], zl[...] = rh, rl
+        rh[...], rl[...] = halves(r_buf[slot])
         for j, p in enumerate(range(0, n, BLOCK)):
             e = p + BLOCK
-            zf[:, p:e] = dot3((zh[:, :e], zl[:, :e]), (wh[p:e, :e], wl[p:e, :e]), NT)
+            z = dot3((rh[:, :e], rl[:, :e]), (wh[p:e, :e], wl[p:e, :e]), NT)
+            zf[:, p:e] = z
+            yh_buf[slot, :, p:e], yl_buf[slot, :, p:e] = halves(z)
             passing(b, j)
-        per = GROUP // own_ref.shape[0]
-
-        @pl.when(me // per == b)
-        def _():
-            x_ref[...] = zf[pl.ds(pl.multiple_of(lax.rem(me, per) * own_ref.shape[0], own_ref.shape[0]), own_ref.shape[0]), :]
-        rh, rl = halves(zf[...])
-        zh[...], zl[...] = rh, rl
-        for j, p in enumerate(range(0, n, BLOCK)):
-            e = p + BLOCK
-            y = dot3((zh[:, p:], zl[:, p:]), (wh[p:, p:e], wl[p:, p:e]), NN)
-            yh_buf[slot, :, p:e], yl_buf[slot, :, p:e] = halves(y)
-            passing(b, 4 + j)
         for copy in store(b, slot):
             copy.start()
+        per = GROUP // own_ref.shape[0]
+
+        @pl.when(me // per == b)
+        def _():
+            x_ref[...] = zf[pl.ds(pl.multiple_of(lax.rem(me, per) * own_ref.shape[0], own_ref.shape[0]), own_ref.shape[0]), :]
         return carry
     lax.fori_loop(0, blocks, transform, 0)
-    transfers(exchange, len(POINTS) - 1)
+    for point in range(nb + 1 + STEPS * blocks, len(POINTS)):
+        transfers(exchange, point)
     exchange.finish_cols()
-    ch_ref[...], cl_ref[...] = halves(cols_ref[...])
+    ch[...], cl[...] = halves(cols_ref[...])
+    saves = []
+    for j, p in enumerate(range(0, n, BLOCK)):
+        e = p + BLOCK
+        z = dot3((ch[:, :e], cl[:, :e]), (wh[p:e, :e], wl[p:e, :e]), NT)
+        zh_buf[:, p:e], zl_buf[:, p:e] = halves(z)
+        saves += [pltpu.make_async_copy(zh_buf.at[:, p:e], zh_ref.at[:, p:e], sem_z.at[j, 0]),
+                  pltpu.make_async_copy(zl_buf.at[:, p:e], zl_ref.at[:, p:e], sem_z.at[j, 1])]
+        saves[-2].start()
+        saves[-1].start()
     exchange.finish()
     for b in (blocks - 2, blocks - 1):
         for copy in store(b, b % 2):
             copy.wait()
+    for copy in [save_l] + saves:
+        copy.wait()
 
 
 def factor(front_diag, own, cols):
@@ -467,6 +480,7 @@
     n = front_diag.shape[0]
     rows = lax.axis_size("col") * own.shape[0]
     vm, anywhere = pl.BlockSpec(memory_space=pltpu.VMEM), pl.BlockSpec(memory_space=pl.ANY)
+    hbm = pl.BlockSpec(memory_space=pl.ANY)
     dma = pltpu.SemaphoreType.DMA
     return pl.pallas_call(
         factor_kernel,
@@ -479,17 +493,20 @@
             jax.ShapeDtypeStruct((cols, n), bf),
             jax.ShapeDtypeStruct((rows, n), f32),
         ),
-        in_specs=[anywhere, vm],
-        out_specs=(vm, vm, anywhere, anywhere, vm, vm, anywhere),
+        in_specs=[hbm, hbm],
+        out_specs=(anywhere, vm, hbm, hbm, anywhere, anywhere, hbm),
         scratch_shapes=[
-            pltpu.VMEM((n, n), f32), pltpu.VMEM((128, n), f32),
+            pltpu.VMEM((n, n), f32), pltpu.VMEM((n, n), f32), pltpu.VMEM((128, n), f32),
             pltpu.VMEM((128, 128), f32), pltpu.VMEM((128, 128), f32), pltpu.VMEM((128, 128), f32),
             pltpu.VMEM((cols, n), f32),
             pltpu.VMEM((n, n), bf), pltpu.VMEM((n, n), bf),
             pltpu.VMEM((2, GROUP, n), f32), pltpu.VMEM((GROUP, n), f32),
             pltpu.VMEM((GROUP, n), bf), pltpu.VMEM((GROUP, n), bf),
             pltpu.VMEM((2, GROUP, n), bf), pltpu.VMEM((2, GROUP, n), bf),
-            dma, dma, dma((2,)), dma((2, 2)),
+            pltpu.VMEM((cols, n), bf), pltpu.VMEM((cols, n), bf),
+            pltpu.VMEM((cols, n), bf), pltpu.VMEM((cols, n), bf),
+            pltpu.VMEM(own.shape, f32),
+            dma, dma, dma, dma((2,)), dma((2, 2)), dma((n // BLOCK, 2)),
             dma((64,)), dma((64,)), dma((32,)), dma((32,)), dma((32,)), dma((32,)),
         ],
         compiler_params=pltpu.CompilerParams(vmem_limit_bytes=56 << 20, collective_id=0, has_side_effects=True),
@@ -497,45 +514,97 @@
     )(front_diag, own)
 
 
-def update_kernel(keep_ref, rh_ref, rl_ref, ch_ref, cl_ref, t_ref, l_ref, x_ref, o_ref, lo_ref, xo_ref):
-    i = pl.program_id(0)
-    lo_ref[...] = l_ref[...]
-    xo_ref[...] = x_ref[...]
-    cols = o_ref.shape[1] // BLOCK
-    for j in range(cols):
-        part = slice(j * BLOCK, (j + 1) * BLOCK)
-        kept = keep_ref[i * cols + j] != 0
-
-        @pl.when(kept)
-        def _():
-            d = dot3((rh_ref[...], rl_ref[...]), (ch_ref[part, :], cl_ref[part, :]), NT)
-            o_ref[:, part] = t_ref[:, part] - d
-
-        @pl.when(jnp.logical_not(kept))
-        def _():
-            o_ref[:, part] = t_ref[:, part]
-
-
-def update(keep, rh, rl, ch, cl, trailing, diag_factor, panel_factor):
+UNIT = 2
+AHEAD = 2
+
+
+def update_kernel(keep_ref, yh_ref, yl_ref, zh_ref, zl_ref, t_ref, l_ref, x_ref, o_ref, lo_ref, xo_ref,
+                  yh, yl, zh, zl, t, l, x, sem_z, sem_in, sem_out, sem_l):
+    n = t.shape[1]
+    size = UNIT * BLOCK
+    steps, cols = t.shape[0] // size, n // BLOCK
+
+    def inputs(i):
+        part = slice(i * size, (i + 1) * size)
+        return [pltpu.make_async_copy(a.at[part], b.at[part], sem_in.at[i, k])
+                for k, (a, b) in enumerate(((yh_ref, yh), (yl_ref, yl), (t_ref, t)))]
+    factors = [pltpu.make_async_copy(zh_ref, zh, sem_z.at[0]), pltpu.make_async_copy(zl_ref, zl, sem_z.at[1])]
+    passed = [pltpu.make_async_copy(l_ref, l, sem_l.at[0]), pltpu.make_async_copy(x_ref, x, sem_l.at[1])]
+    passed_on = [pltpu.make_async_copy(l, lo_ref, sem_l.at[2]), pltpu.make_async_copy(x, xo_ref, sem_l.at[3])]
+    outputs = []
+    for copy in factors:
+        copy.start()
+    for i in range(AHEAD):
+        for copy in inputs(i):
+            copy.start()
+    for copy in factors:
+        copy.wait()
+    for i in range(steps):
+        if i + AHEAD < steps:
+            for copy in inputs(i + AHEAD):
+                copy.start()
+        if i + AHEAD == steps:
+            for copy in passed:
+                copy.start()
+        for copy in inputs(i):
+            copy.wait()
+        base = i * UNIT * cols
+        kept = [keep_ref[base + k] for k in range(UNIT * cols)]
+        many = sum(kept) > UNIT * cols // 2
+
+        @pl.when(many)
+        def _():
+            rows = slice(i * size, (i + 1) * size)
+            for j in range(cols):
+                part = slice(j * BLOCK, (j + 1) * BLOCK)
+                d = dot3((yh[rows, :], yl[rows, :]), (zh[part, :], zl[part, :]), NT)
+                for r in range(UNIT):
+                    at = slice(i * size + r * BLOCK, i * size + (r + 1) * BLOCK)
+                    t[at, part] -= jnp.where(kept[r * cols + j] != 0, d[r * BLOCK:(r + 1) * BLOCK], 0.0)
+
+        @pl.when(jnp.logical_not(many))
+        def _():
+            def block(k, carry):
+                rows = pl.ds(pl.multiple_of(i * size + k // cols * BLOCK, BLOCK), BLOCK)
+                part = pl.ds(pl.multiple_of(k % cols * BLOCK, BLOCK), BLOCK)
+
+                @pl.when(keep_ref[base + k] != 0)
+                def _():
+                    t[rows, part] -= dot3((yh[rows, :], yl[rows, :]), (zh[part, :], zl[part, :]), NT)
+                return carry
+            lax.fori_loop(0, UNIT * cols, block, 0)
+        rows = slice(i * size, (i + 1) * size)
+        outputs.append(pltpu.make_async_copy(t.at[rows], o_ref.at[rows], sem_out.at[i]))
+        outputs[-1].start()
+        if i == steps - 2:
+            for copy in passed:
+                copy.wait()
+            for copy in passed_on:
+                copy.start()
+    for copy in outputs + passed_on:
+        copy.wait()
+
+
+def update(keep, yh, yl, zh, zl, trailing, diag_factor, panel_factor):
+    f32, bf = jnp.float32, jnp.bfloat16
     m, n = trailing.shape
-    k = rh.shape[1]
-    steps = m // BLOCK
-    row = lambda size, width: pl.BlockSpec((size, width), lambda i, s: (i, 0))
-    whole = lambda size, width: pl.BlockSpec((size, width), lambda i, s: (0, 0))
-    ld, lx = diag_factor.shape[0] // steps, panel_factor.shape[0] // steps
+    steps = m // (UNIT * BLOCK)
+    anywhere, hbm = pl.BlockSpec(memory_space=pl.ANY), pl.BlockSpec(memory_space=pl.ANY)
+    dma = pltpu.SemaphoreType.DMA
     return pl.pallas_call(
         update_kernel,
-        out_shape=(jax.ShapeDtypeStruct((m, n), jnp.float32), jax.ShapeDtypeStruct(diag_factor.shape, jnp.float32),
-                   jax.ShapeDtypeStruct(panel_factor.shape, jnp.float32)),
-        grid_spec=pltpu.PrefetchScalarGridSpec(
-            num_scalar_prefetch=1,
-            grid=(steps,),
-            in_specs=[row(BLOCK, k), row(BLOCK, k), whole(n, k), whole(n, k), row(BLOCK, n), row(ld, k), row(lx, k)],
-            out_specs=(row(BLOCK, n), row(ld, k), row(lx, k)),
-        ),
+        out_shape=(jax.ShapeDtypeStruct((m, n), f32), jax.ShapeDtypeStruct(diag_factor.shape, f32),
+                   jax.ShapeDtypeStruct(panel_factor.shape, f32)),
+        in_specs=[pl.BlockSpec(memory_space=pltpu.SMEM), hbm, hbm, anywhere, anywhere, hbm, anywhere, anywhere],
+        out_specs=(hbm,) * 3,
+        scratch_shapes=[
+            pltpu.VMEM(yh.shape, bf), pltpu.VMEM(yl.shape, bf), pltpu.VMEM(zh.shape, bf), pltpu.VMEM(zl.shape, bf),
+            pltpu.VMEM((m, n), f32), pltpu.VMEM(diag_factor.shape, f32), pltpu.VMEM(panel_factor.shape, f32),
+            dma((2,)), dma((steps, 3)), dma((steps,)), dma((4,)),
+        ],
         compiler_params=pltpu.CompilerParams(vmem_limit_bytes=60 << 20),
         name="update",
-    )(keep, rh, rl, ch, cl, trailing, diag_factor, panel_factor)
+    )(keep, yh, yl, zh, zl, trailing, diag_factor, panel_factor)
 
 
 def local(front_diag, panel_rows, trailing, pattern):
@@ -543,8 +612,8 @@
     row_index = lax.axis_index("row") * row_blocks + jnp.arange(row_blocks)
     col_index = lax.axis_index("col") * col_blocks + jnp.arange(col_blocks)
     keep = pattern * (row_index[:, None] >= col_index[None, :]).astype(jnp.int32)
-    diag_factor, panel_factor, yh, yl, ch, cl, _ = factor(front_diag, panel_rows, trailing.shape[1])
-    schur, diag_factor, panel_factor = update(keep.reshape(-1), yh, yl, ch, cl, trailing, diag_factor, panel_factor)
+    diag_factor, panel_factor, yh, yl, zh, zl, _ = factor(front_diag, panel_rows, trailing.shape[1])
+    schur, diag_factor, panel_factor = update(keep.reshape(-1), yh, yl, zh, zl, trailing, diag_factor, panel_factor)
     return (diag_factor, panel_factor, schur)
 
 

time: 121 us -> 111 us (0.917)
  the two profiles are of different devices: /device:TPU:34 before, /device:TPU:99 now
where the time goes in v4:
time: 111 us; the launch traced here: 110 us
  Pallas kernels  108 us (97%)
    pallas_call x1, Pallas kernels, factor(): pl.pallas_call(factor_kernel, out_shape=(jax.ShapeDtypeStruct((n, n), f32...  87.8 us
    pallas_call x1, Pallas kernels, update(): pl.pallas_call(update_kernel, out_shape=(jax.ShapeDtypeStruct((m, n), f32...  20.3 us

profile of v4, /device:TPU:99, one launch (start us, length us, event | category | flops | bytes accessed | tf_op | source)
XLA Modules:
  0.0 110.4 jit_solution(2783950369059895824)
XLA Ops:
  0.7 0.8 compare_select_fusion
  1.4 0.1 copy.8
  1.5 0.6 reshape.17.keep_ref
  2.1 87.8 %factor.1 = (f32[1024,1024]{1,0:T(8,128)}, f32[128,1024]{1,0:T(8,128)}, bf16[2048,1024]{1,0:T(8,128)(2,1)}, bf16[2048,1024]{1,0:T(8,128)(2,1)}, bf16[1024,1024]{...) custom-call(f32[1024,1024]{1,0:T(8,128)} %a_ref.1, f32[128,1024]{1,0:T(8,128)} %own_in.1), custom_call_target="tpu_custom_call" | custom-call | tf_op jit(solution)/shard_map/factor/pallas_call | solution.py:485
  89.9 20.3 %update.1 = (f32[2048,1024]{1,0:T(8,128)}, f32[1024,1024]{1,0:T(8,128)}, f32[128,1024]{1,0:T(8,128)}) custom-call(s32[32]{0:T(128)} %reshape.17.keep_ref, bf16[2048,1024]{1,0:T(8,128)(2,1)} %get-tuple-element.12.yh_ref, bf16[2048,1024]{1,0:T(8,128)(2,1)} %get-tuple-element.13.yl_ref, bf16[1024,1024]{1,0:T(8,128)(2,1)} %get-tuple-element.14.zh_ref, ...), custom_call_target="tpu_custom_call" | custom-call | tf_op jit(solution)/shard_map/update/pallas_call | solution.py:594
  (2 shorter events, 0.0 us)

commit v5 on v4

--- a/solution.py
+++ b/solution.py
@@ -167,7 +167,8 @@
         ((2, 0), (0, 1), (0, 3)),
         ((1, 1), (1, 3), (3, 1), (3, 3)),
         ((2, 1), (2, 3), (0, 2)),
-        ((1, 2), (3, 2), (2, 2)),
+        ((1, 2), (3, 2)),
+        ((2, 2),),
     )
 
     def col_slot(self, h, a, b):
@@ -268,10 +269,21 @@
         def _():
             self.across(h, a, b, False).start()
 
-    def finish_cols(self):
+    def own_row(self):
+        return self.y // 2 == lax.rem(self.x, 2)
+
+    def early_half(self):
+        return jnp.where(self.own_row(), lax.rem(self.y, 2), 1 - lax.rem(self.y, 2))
+
+    def finish_cols(self, early):
         for wave in range(len(self.ARRIVALS)):
             for h, a, b in self.pieces(wave):
+                dy = b if h == 0 else a
+                if dy == (2 if early else 0):
+                    continue
                 inside = self.in_cols(h, a, b) & self.needed()
+                if dy % 2 == 1:
+                    inside = inside & (jnp.logical_not(self.own_row()) if early else self.own_row())
 
                 @pl.when(inside & self.holder() & (self.z == self.y))
                 def _():
@@ -297,7 +309,7 @@
                     self.along(h, a, b, False).wait_send()
 
 
-ROW_POINTS = (0, 1, 3, 5, 6, 8)
+ROW_POINTS = (0, 1, 3, 5, 6, 7, 8)
 STEPS = 4
 POINTS = [0.0] + [2.5 + 5.6 * (k + 1) for k in range(8)] + [49.5 + 0.65 * i for i in range(16)] + [60.5 + 0.7 * i for i in range(40)]
 
@@ -324,13 +336,13 @@
 RELAYS = relay_points()
 
 
-def transfers(exchange, point):
+def transfers(exchange, point, near=False, far=False):
     for wave, at in enumerate(ROW_POINTS):
         if at == point:
             exchange.start_rows(wave)
             exchange.start_cols(wave)
     for (h, a, b, hop), at in RELAYS.items():
-        if at == point:
+        if at == point and not (near and (a, b) == (2, 2)) and not (far and (a, b) != (2, 2)):
             exchange.relay_cols(h, a, b, hop)
 
 
@@ -372,6 +384,7 @@
         l_ref[pl.ds(oq, 128), pl.ds(oq, 128)] = u_ref[...].T
         if last:
             w_ref[pl.ds(oq, 128), pl.ds(oq, 128)] = wd
+            wh[pl.ds(oq, 128), :], wl[pl.ds(oq, 128), :] = halves(w_ref[pl.ds(oq, 128), :])
             return
         g_ref[...] = g
         g_ref[:, pl.ds(oq, 128)] += wd
@@ -381,6 +394,8 @@
             l_ref[i * 128:(i + 1) * 128, pl.ds(oq, 128)] = jnp.where(q < i, li, l_ref[i * 128:(i + 1) * 128, pl.ds(oq, 128)])
             w_ref[i * 128:(i + 1) * 128, :] -= dot6(wide_left(li), right)
         w_ref[pl.ds(oq, 128), pl.ds(oq, 128)] = jnp.where(p > 0, wd, w_ref[pl.ds(oq, 128), pl.ds(oq, 128)])
+        wh[pl.ds(oq, 128), :], wl[pl.ds(oq, 128), :] = halves(done)
+        wh[pl.ds(oq, 128), pl.ds(oq, 128)], wl[pl.ds(oq, 128), pl.ds(oq, 128)] = halves(wd)
 
     def panel(p, carry):
         o = pl.multiple_of(p * 128, 128)
@@ -416,7 +431,6 @@
     settle(nb, True)
     save_l = pltpu.make_async_copy(l_ref, l_out, sem_l)
     save_l.start()
-    wh[...], wl[...] = halves(w_ref[...])
 
     def passing(b, j):
         for k in range(blocks):
@@ -454,19 +468,30 @@
             x_ref[...] = zf[pl.ds(pl.multiple_of(lax.rem(me, per) * own_ref.shape[0], own_ref.shape[0]), own_ref.shape[0]), :]
         return carry
     lax.fori_loop(0, blocks, transform, 0)
+    late = sorted({at for (h, a, b, hop), at in RELAYS.items() if (a, b) == (2, 2) and at >= nb + 1 + STEPS * blocks})
     for point in range(nb + 1 + STEPS * blocks, len(POINTS)):
-        transfers(exchange, point)
-    exchange.finish_cols()
-    ch[...], cl[...] = halves(cols_ref[...])
+        transfers(exchange, point, near=True)
     saves = []
-    for j, p in enumerate(range(0, n, BLOCK)):
-        e = p + BLOCK
-        z = dot3((ch[:, :e], cl[:, :e]), (wh[p:e, :e], wl[p:e, :e]), NT)
-        zh_buf[:, p:e], zl_buf[:, p:e] = halves(z)
-        saves += [pltpu.make_async_copy(zh_buf.at[:, p:e], zh_ref.at[:, p:e], sem_z.at[j, 0]),
-                  pltpu.make_async_copy(zl_buf.at[:, p:e], zl_ref.at[:, p:e], sem_z.at[j, 1])]
-        saves[-2].start()
-        saves[-1].start()
+    size = cols_ref.shape[0] // 2
+
+    def column_factor(early):
+        exchange.finish_cols(early)
+        half = exchange.early_half() if early else 1 - exchange.early_half()
+        part = pl.ds(pl.multiple_of(half * size, size), size)
+        ch[...], cl[...] = halves(cols_ref[part, :])
+        for j, p in enumerate(range(0, n, BLOCK)):
+            e = p + BLOCK
+            z = dot3((ch[:, :e], cl[:, :e]), (wh[p:e, :e], wl[p:e, :e]), NT)
+            zh_buf[part, p:e], zl_buf[part, p:e] = halves(z)
+            for k, (a, b) in enumerate(((zh_buf, zh_ref), (zl_buf, zl_ref))):
+                saves.append(pltpu.make_async_copy(a.at[part, p:e], b.at[part, p:e], sem_z.at[int(early), j, k]))
+                saves[-1].start()
+            if early and j % 2 == 1 and late:
+                transfers(exchange, late.pop(0), far=True)
+    column_factor(True)
+    for point in late:
+        transfers(exchange, point, far=True)
+    column_factor(False)
     exchange.finish()
     for b in (blocks - 2, blocks - 1):
         for copy in store(b, b % 2):
@@ -503,10 +528,10 @@
             pltpu.VMEM((2, GROUP, n), f32), pltpu.VMEM((GROUP, n), f32),
             pltpu.VMEM((GROUP, n), bf), pltpu.VMEM((GROUP, n), bf),
             pltpu.VMEM((2, GROUP, n), bf), pltpu.VMEM((2, GROUP, n), bf),
-            pltpu.VMEM((cols, n), bf), pltpu.VMEM((cols, n), bf),
+            pltpu.VMEM((cols // 2, n), bf), pltpu.VMEM((cols // 2, n), bf),
             pltpu.VMEM((cols, n), bf), pltpu.VMEM((cols, n), bf),
             pltpu.VMEM(own.shape, f32),
-            dma, dma, dma, dma((2,)), dma((2, 2)), dma((n // BLOCK, 2)),
+            dma, dma, dma, dma((2,)), dma((2, 2)), dma((2, n // BLOCK, 2)),
             dma((64,)), dma((64,)), dma((32,)), dma((32,)), dma((32,)), dma((32,)),
         ],
         compiler_params=pltpu.CompilerParams(vmem_limit_bytes=56 << 20, collective_id=0, has_side_effects=True),
@@ -518,11 +543,16 @@
 AHEAD = 2
 
 
-def update_kernel(keep_ref, yh_ref, yl_ref, zh_ref, zl_ref, t_ref, l_ref, x_ref, o_ref, lo_ref, xo_ref,
+def update_kernel(pattern_ref, yh_ref, yl_ref, zh_ref, zl_ref, t_ref, l_ref, x_ref, o_ref, lo_ref, xo_ref,
                   yh, yl, zh, zl, t, l, x, sem_z, sem_in, sem_out, sem_l):
     n = t.shape[1]
     size = UNIT * BLOCK
     steps, cols = t.shape[0] // size, n // BLOCK
+    first_row = lax.axis_index("row") * (steps * UNIT)
+    first_col = lax.axis_index("col") * cols
+
+    def keep(r, c):
+        return (pattern_ref[c, r] != 0) & (first_row + r >= first_col + c)
 
     def inputs(i):
         part = slice(i * size, (i + 1) * size)
@@ -548,9 +578,8 @@
                 copy.start()
         for copy in inputs(i):
             copy.wait()
-        base = i * UNIT * cols
-        kept = [keep_ref[base + k] for k in range(UNIT * cols)]
-        many = sum(kept) > UNIT * cols // 2
+        kept = [keep(i * UNIT + k // cols, k % cols) for k in range(UNIT * cols)]
+        many = sum(k.astype(jnp.int32) for k in kept) > UNIT * cols // 2
 
         @pl.when(many)
         def _():
@@ -560,7 +589,7 @@
                 d = dot3((yh[rows, :], yl[rows, :]), (zh[part, :], zl[part, :]), NT)
                 for r in range(UNIT):
                     at = slice(i * size + r * BLOCK, i * size + (r + 1) * BLOCK)
-                    t[at, part] -= jnp.where(kept[r * cols + j] != 0, d[r * BLOCK:(r + 1) * BLOCK], 0.0)
+                    t[at, part] -= jnp.where(kept[r * cols + j], d[r * BLOCK:(r + 1) * BLOCK], 0.0)
 
         @pl.when(jnp.logical_not(many))
         def _():
@@ -568,7 +597,7 @@
                 rows = pl.ds(pl.multiple_of(i * size + k // cols * BLOCK, BLOCK), BLOCK)
                 part = pl.ds(pl.multiple_of(k % cols * BLOCK, BLOCK), BLOCK)
 
-                @pl.when(keep_ref[base + k] != 0)
+                @pl.when(keep(i * UNIT + k // cols, k % cols))
                 def _():
                     t[rows, part] -= dot3((yh[rows, :], yl[rows, :]), (zh[part, :], zl[part, :]), NT)
                 return carry
@@ -585,7 +614,7 @@
         copy.wait()
 
 
-def update(keep, yh, yl, zh, zl, trailing, diag_factor, panel_factor):
+def update(pattern, yh, yl, zh, zl, trailing, diag_factor, panel_factor):
     f32, bf = jnp.float32, jnp.bfloat16
     m, n = trailing.shape
     steps = m // (UNIT * BLOCK)
@@ -604,16 +633,12 @@
         ],
         compiler_params=pltpu.CompilerParams(vmem_limit_bytes=60 << 20),
         name="update",
-    )(keep, yh, yl, zh, zl, trailing, diag_factor, panel_factor)
+    )(pattern, yh, yl, zh, zl, trailing, diag_factor, panel_factor)
 
 
 def local(front_diag, panel_rows, trailing, pattern):
-    row_blocks, col_blocks = pattern.shape
-    row_index = lax.axis_index("row") * row_blocks + jnp.arange(row_blocks)
-    col_index = lax.axis_index("col") * col_blocks + jnp.arange(col_blocks)
-    keep = pattern * (row_index[:, None] >= col_index[None, :]).astype(jnp.int32)
     diag_factor, panel_factor, yh, yl, zh, zl, _ = factor(front_diag, panel_rows, trailing.shape[1])
-    schur, diag_factor, panel_factor = update(keep.reshape(-1), yh, yl, zh, zl, trailing, diag_factor, panel_factor)
+    schur, diag_factor, panel_factor = update(pattern.T, yh, yl, zh, zl, trailing, diag_factor, panel_factor)
     return (diag_factor, panel_factor, schur)
 
 

time: 111 us -> 105 us (0.946)
  Pallas kernels: 108 us -> 103 us
    pallas_call x1, Pallas kernels: 20.3 us -> 17.6 us  [update(): pl.pallas_call(update_kernel, out_shape=(jax.ShapeDtypeStruct((m, n), f32...]
    pallas_call x1, Pallas kernels: 87.8 us -> 85.8 us  [factor(): pl.pallas_call(factor_kernel, out_shape=(jax.ShapeDtypeStruct((n, n), f32...]
where the time goes in v5:
time: 105 us; the launch traced here: 104 us
  Pallas kernels  103 us (98%)
    pallas_call x1, Pallas kernels, factor(): pl.pallas_call(factor_kernel, out_shape=(jax.ShapeDtypeStruct((n, n), f32...  85.8 us
    pallas_call x1, Pallas kernels, update(): pl.pallas_call(update_kernel, out_shape=(jax.ShapeDtypeStruct((m, n), f32...  17.6 us

profile of v5, /device:TPU:99, one launch (start us, length us, event | category | flops | bytes accessed | tf_op | source)
XLA Modules:
  0.0 104.2 jit_solution(16484884619246292555)
XLA Ops:
  0.6 85.8 %factor.1 = (f32[1024,1024]{1,0:T(8,128)}, f32[128,1024]{1,0:T(8,128)}, bf16[2048,1024]{1,0:T(8,128)(2,1)}, bf16[2048,1024]{1,0:T(8,128)(2,1)}, bf16[1024,1024]{...) custom-call(f32[1024,1024]{1,0:T(8,128)} %a_ref.1, f32[128,1024]{1,0:T(8,128)} %own_in.1), custom_call_target="tpu_custom_call" | custom-call | tf_op jit(solution)/shard_map/factor/pallas_call | solution.py:510
  86.4 17.6 %update.1 = (f32[2048,1024]{1,0:T(8,128)}, f32[1024,1024]{1,0:T(8,128)}, f32[128,1024]{1,0:T(8,128)}) custom-call(s32[4,8]{1,0:T(4,128)} %bitcast.1, bf16[2048,1024]{1,0:T(8,128)(2,1)} %get-tuple-element.12.yh_ref, bf16[2048,1024]{1,0:T(8,128)(2,1)} %get-tuple-element.13.yl_ref, bf16[1024,1024]{1,0:T(8,128)(2,1)} %get-tuple-element.14.zh_ref, ...), custom_call_target="tpu_custom_call" | custom-call | tf_op jit(solution)/shard_map/update/pallas_call | solution.py:623

commit v6 on v5

--- a/solution.py
+++ b/solution.py
@@ -559,25 +559,32 @@
         return [pltpu.make_async_copy(a.at[part], b.at[part], sem_in.at[i, k])
                 for k, (a, b) in enumerate(((yh_ref, yh), (yl_ref, yl), (t_ref, t)))]
     factors = [pltpu.make_async_copy(zh_ref, zh, sem_z.at[0]), pltpu.make_async_copy(zl_ref, zl, sem_z.at[1])]
-    passed = [pltpu.make_async_copy(l_ref, l, sem_l.at[0]), pltpu.make_async_copy(x_ref, x, sem_l.at[1])]
-    passed_on = [pltpu.make_async_copy(l, lo_ref, sem_l.at[2]), pltpu.make_async_copy(x, xo_ref, sem_l.at[3])]
+    bands = l.shape[0] // BLOCK
+    lower = [(slice(q * BLOCK, (q + 1) * BLOCK), slice(0, (q + 1) * BLOCK)) for q in range(bands)]
+    passed = [pltpu.make_async_copy(l_ref.at[at], l.at[at], sem_l.at[q]) for q, at in enumerate(lower)]
+    passed.append(pltpu.make_async_copy(x_ref, x, sem_l.at[bands]))
+    passed_on = [pltpu.make_async_copy(l, lo_ref, sem_l.at[bands + 1]), pltpu.make_async_copy(x, xo_ref, sem_l.at[bands + 2])]
     outputs = []
     for copy in factors:
         copy.start()
-    for i in range(AHEAD):
+    for copy in inputs(0):
+        copy.start()
+    for q in range(bands - 1):
+        l[q * BLOCK:(q + 1) * BLOCK, (q + 1) * BLOCK:] = jnp.zeros((BLOCK, l.shape[1] - (q + 1) * BLOCK), jnp.float32)
+    for copy in factors:
+        copy.wait()
+    for i in range(1, AHEAD):
         for copy in inputs(i):
             copy.start()
-    for copy in factors:
-        copy.wait()
     for i in range(steps):
+        for copy in inputs(i):
+            copy.wait()
         if i + AHEAD < steps:
             for copy in inputs(i + AHEAD):
                 copy.start()
         if i + AHEAD == steps:
             for copy in passed:
                 copy.start()
-        for copy in inputs(i):
-            copy.wait()
         kept = [keep(i * UNIT + k // cols, k % cols) for k in range(UNIT * cols)]
         many = sum(k.astype(jnp.int32) for k in kept) > UNIT * cols // 2
 
@@ -629,7 +636,7 @@
         scratch_shapes=[
             pltpu.VMEM(yh.shape, bf), pltpu.VMEM(yl.shape, bf), pltpu.VMEM(zh.shape, bf), pltpu.VMEM(zl.shape, bf),
             pltpu.VMEM((m, n), f32), pltpu.VMEM(diag_factor.shape, f32), pltpu.VMEM(panel_factor.shape, f32),
-            dma((2,)), dma((steps, 3)), dma((steps,)), dma((4,)),
+            dma((2,)), dma((steps, 3)), dma((steps,)), dma((diag_factor.shape[0] // BLOCK + 3,)),
         ],
         compiler_params=pltpu.CompilerParams(vmem_limit_bytes=60 << 20),
         name="update",

time: 105 us -> 105 us (level)
  no operation moved by 1% of the time
where the time goes in v6:
time: 105 us; the launch traced here: 104 us
  Pallas kernels  103 us (98%)
    pallas_call x1, Pallas kernels, factor(): pl.pallas_call(factor_kernel, out_shape=(jax.ShapeDtypeStruct((n, n), f32...  85.8 us
    pallas_call x1, Pallas kernels, update(): pl.pallas_call(update_kernel, out_shape=(jax.ShapeDtypeStruct((m, n), f32...  17.1 us

profile of v6, /device:TPU:99, one launch (start us, length us, event | category | flops | bytes accessed | tf_op | source)
XLA Modules:
  0.0 103.7 jit_solution(16544530693860927755)
XLA Ops:
  0.6 85.8 %factor.1 = (f32[1024,1024]{1,0:T(8,128)}, f32[128,1024]{1,0:T(8,128)}, bf16[2048,1024]{1,0:T(8,128)(2,1)}, bf16[2048,1024]{1,0:T(8,128)(2,1)}, bf16[1024,1024]{...) custom-call(f32[1024,1024]{1,0:T(8,128)} %a_ref.1, f32[128,1024]{1,0:T(8,128)} %own_in.1), custom_call_target="tpu_custom_call" | custom-call | tf_op jit(solution)/shard_map/factor/pallas_call | solution.py:510
  86.4 17.1 %update.1 = (f32[2048,1024]{1,0:T(8,128)}, f32[1024,1024]{1,0:T(8,128)}, f32[128,1024]{1,0:T(8,128)}) custom-call(s32[4,8]{1,0:T(4,128)} %bitcast.1, bf16[2048,1024]{1,0:T(8,128)(2,1)} %get-tuple-element.12.yh_ref, bf16[2048,1024]{1,0:T(8,128)(2,1)} %get-tuple-element.13.yl_ref, bf16[1024,1024]{1,0:T(8,128)(2,1)} %get-tuple-element.14.zh_ref, ...), custom_call_target="tpu_custom_call" | custom-call | tf_op jit(solution)/shard_map/update/pallas_call | solution.py:630
